TPU v7x, 32 devices: a whole 2x2x4 slice. The times are simulated.
32 devices in a mesh: dp: 8 (over z, y), ctx: 4 (over x, core).
Axes of the slice: x: 2, y: 2, z: 4, core: 2. Of those that a mesh axis runs over, the one named last changes fastest.
Arguments:
- tokens: bfloat16 [8, 512, 2048], P('dp', 'ctx'), may hold values from -6 to 6
- segment_ids: int32 [8, 512], P('dp', 'ctx'), may hold values from 0 to 2, as said below
- positions: int32 [8, 512], P('dp', 'ctx'), may hold values from 0 to 511, as said below
- attn_gain: bfloat16 [2048], P(('dp', 'ctx')), may hold values from 0.5 to 1.5
- w_query: bfloat16 [2048, 2048], P(('dp', 'ctx')), may hold values from -0.125 to 0.125
- w_key: bfloat16 [2048, 512], P(('dp', 'ctx')), may hold values from -0.125 to 0.125
- w_value: bfloat16 [2048, 512], P(('dp', 'ctx')), may hold values from -0.125 to 0.125
- w_output: bfloat16 [2048, 2048], P(('dp', 'ctx')), may hold values from -1 to 1
- ffn_gain: bfloat16 [2048], P(('dp', 'ctx')), may hold values from 0.5 to 1.5
- w_gate: bfloat16 [2048, 8192], P('dp', 'ctx'), may hold values from -0.125 to 0.125
- w_up: bfloat16 [2048, 8192], P('dp', 'ctx'), may hold values from -0.125 to 0.125
- w_down: bfloat16 [8192, 2048], P('ctx', 'dp'), may hold values from -0.125 to 0.125
- cotangent: bfloat16 [8, 512, 2048], P('dp', 'ctx'), may hold values from -6 to 6
Outputs:
- mixed: bfloat16 [8, 512, 2048], P('dp', 'ctx')
- grad_tokens: float32 [8, 512, 2048], P('dp', 'ctx')
- grad_attn_gain: float32 [2048], P(('dp', 'ctx'))
- grad_query: float32 [2048, 2048], P(('dp', 'ctx'))
- grad_key: float32 [2048, 512], P(('dp', 'ctx'))
- grad_value: float32 [2048, 512], P(('dp', 'ctx'))
- grad_output: float32 [2048, 2048], P(('dp', 'ctx'))
- grad_ffn_gain: float32 [2048], P(('dp', 'ctx'))
- grad_gate: float32 [2048, 8192], P('dp', 'ctx')
- grad_up: float32 [2048, 8192], P('dp', 'ctx')
- grad_down: float32 [8192, 2048], P('ctx', 'dp')
Inputs may be any that keep to these rules, and one draw needn't show every extreme that they name: `segment_ids`: along each packed sequence of 512 tokens the document number never falls and starts at 0; documents do not cross sequences. `positions`: 0 at a document's first token and rising by one along the document; the first packed sequence holds a single document.
All inputs are finite; a program needn't handle non-finite values.
Results may differ from a plain program's by a relative error of at most 0.018.
Values may be sent and summed in bfloat16 or wider, within the bound.
No kernel may reach another device: no remote copies, remote signals or barrier semaphores. Data moves between devices by JAX's collectives and lax.ppermute only.
A program may use at most 256 MiB of HBM per device.

v0:
```python
import jax
import jax.numpy as jnp
from jax import lax
from jax.sharding import Mesh
from jax.sharding import PartitionSpec as P


QUERY_HEADS = 32
KEY_VALUE_HEADS = 8
HEAD_WIDTH = 64


EPS_NORM = 1e-05
ROPE_BASE = 500000.0
MASKED = -1e30


F32 = jnp.float32
BF16 = jnp.bfloat16


def rope_tables(where_pos, half_width):
    freqs = ROPE_BASE ** (-(jnp.arange(half_width, dtype=jnp.float32) / half_width))
    angles = where_pos.astype(jnp.float32)[..., None] * freqs
    return (jnp.cos(angles), jnp.sin(angles))


def apply_rotation(values, cosine_table, sine_table):
    half_width = values.shape[-1] // 2
    first = values[..., :half_width]
    second = values[..., half_width:]
    cosine_table = cosine_table[..., None, :]
    sine_table = sine_table[..., None, :]
    return jnp.concatenate(
        [first * cosine_table - second * sine_table, second * cosine_table + first * sine_table],
        axis=-1,
    )


def reverse_rotation(grads, cosine_table, sine_table):
    half_width = grads.shape[-1] // 2
    first = grads[..., :half_width]
    second = grads[..., half_width:]
    cosine_table = cosine_table[..., None, :]
    sine_table = sine_table[..., None, :]
    return jnp.concatenate(
        [first * cosine_table + second * sine_table, second * cosine_table - first * sine_table],
        axis=-1,
    )


def norm_back(upstream, normed, inverse, gain):
    scaled = upstream * gain
    return inverse * (scaled - normed * jnp.mean(scaled * normed, axis=-1, keepdims=True))


def tdot(left, right):
    return lax.dot_general(
        left, right, (((0,), (0,)), ((), ())), preferred_element_type=jnp.float32
    )


def dot_t(left, right):
    return lax.dot_general(
        left, right, (((1,), (1,)), ((), ())), preferred_element_type=jnp.float32
    )


def back(at, step, count):
    return lax.rem(at + (count - step % count), jnp.int32(count))


def ahead(at, step, count):
    return lax.rem(at + step, jnp.int32(count))


def shift(value, axis, step=1):
    count = lax.axis_size(axis)
    return lax.ppermute(value, axis, [(i, (i + step) % count) for i in range(count)])


def gather_ring(value, axis):
    slots = [value]
    for _ in range(lax.axis_size(axis) - 1):
        slots.append(shift(slots[-1], axis))
    return slots


def add_rounded(left, right):
    return (left.astype(F32) + right.astype(F32)).astype(left.dtype)


def reduce_ring(parts, axis):
    count = lax.axis_size(axis)
    if count == 1:
        return parts[0]
    total = parts[1]
    for k in range(2, count):
        total = add_rounded(shift(total, axis), parts[k])
    return add_rounded(shift(total, axis), parts[0])


def gather_tokens(value):
    slots = []
    for piece in gather_ring(value, "z"):
        pair = jnp.concatenate(gather_ring(piece, "x"), axis=0)
        slots.append(jnp.concatenate(gather_ring(pair, "c"), axis=0))
    return slots


def reduce_block(block):
    cores = lax.axis_size("c")
    across = lax.axis_size("x")
    rows = block.shape[0] // cores
    pair = reduce_ring([block[k * rows : (k + 1) * rows] for k in range(cores)], "c")
    rows = rows // across
    return reduce_ring([pair[k * rows : (k + 1) * rows] for k in range(across)], "x")


def reduce_locally(blocks):
    count = len(blocks)
    local = {k % count: reduce_block(blocks[k % count]) for k in range(1, count + 1)}
    return [local[k] for k in range(count)]


def hop_order(slot):
    return ("y", "x", "c") if slot % 2 == 0 else ("x", "y", "c")


def gather_rows(piece, slot):
    for axis in hop_order(slot):
        piece = jnp.concatenate(gather_ring(piece, axis), axis=0)
    return piece


def reduce_axes(block, axes):
    for axis in axes:
        rows = block.shape[-2] // lax.axis_size(axis)
        parts = [block[..., k * rows : (k + 1) * rows, :] for k in range(lax.axis_size(axis))]
        block = reduce_ring(parts, axis)
    return block


def reduce_weight(permuted, upstream):
    count = lax.axis_size("z")
    columns = permuted.shape[1] // count
    local = {}
    for step in range(1, count + 1):
        k = step % count
        part = tdot(permuted[:, k * columns : (k + 1) * columns], upstream).astype(BF16)
        local[k] = reduce_axes(part, reversed(hop_order(k)))
    local = [local[k] for k in range(count)]
    return reduce_ring(local, "z"), local


def rows_product(value, slots):
    rows = slots[0].shape[0]
    total = None
    for k, slot in enumerate(slots):
        part = jnp.dot(value[:, k * rows : (k + 1) * rows], slot, preferred_element_type=F32)
        total = part if total is None else total + part
    return total


def after(values, *waits):
    return lax.optimization_barrier((tuple(values), waits))[0]


def layer(
    tokens,
    segment_ids,
    positions,
    attn_gain,
    w_query,
    w_key,
    w_value,
    w_output,
    ffn_gain,
    w_gate,
    w_up,
    w_down,
    cotangent,
):
    everywhere = ("z", "y", "x", "c")
    size_z, size_y, size_x, size_c = (lax.axis_size(a) for a in everywhere)
    at_z, at_y, at_x, at_c = (lax.axis_index(a) for a in everywhere)
    devices = size_z * size_y * size_x * size_c
    count_ctx = size_x * size_c
    local_sequence, context_rows, width = tokens.shape
    token_rows = local_sequence * context_rows
    sequence_length = context_rows * count_ctx
    query_groups = QUERY_HEADS // KEY_VALUE_HEADS
    query_width = QUERY_HEADS * HEAD_WIDTH
    kv_width = KEY_VALUE_HEADS * HEAD_WIDTH
    factor = 1.0 / HEAD_WIDTH**0.5
    own_rows = w_query.shape[0]

    sizes = {"y": size_y, "x": size_x, "c": size_c}
    here = {"y": at_y, "x": at_x, "c": at_c}
    plane = jnp.arange(devices // size_z, dtype=jnp.int32)
    pieces = []
    for slot in range(size_z):
        stride, at = 1, {}
        for axis in hop_order(slot):
            away = (plane // stride) % sizes[axis]
            at[axis] = lax.rem(here[axis] + sizes[axis] - away, sizes[axis])
            stride *= sizes[axis]
        row = back(at_z, slot, size_z) * size_y + at["y"]
        pieces.append((row * size_x + at["x"]) * size_c + at["c"])
    piece = jnp.concatenate(pieces)
    feature = (piece[:, None] * own_rows + jnp.arange(own_rows, dtype=jnp.int32)).reshape(-1)
    selector = (jnp.arange(width, dtype=jnp.int32)[:, None] == feature[None, :]).astype(BF16)

    def by_distance(value):
        return jnp.dot(value, selector, preferred_element_type=F32).astype(BF16)

    def by_feature(value):
        return dot_t(value.astype(BF16), selector)

    lanes = 128
    qkv_width = query_width + 2 * kv_width
    gain_columns = jnp.pad(jnp.stack([attn_gain, ffn_gain], axis=1), ((0, 0), (0, lanes - 2)))
    qkv_own = jnp.concatenate([w_query, w_key, w_value, gain_columns], axis=1)
    qkv_ring = gather_ring(qkv_own, "z")
    packed_slots = [gather_rows(part, k) for k, part in enumerate(qkv_ring)]
    slot_rows = width // size_z
    qkv_slots = [part[:, :qkv_width] for part in packed_slots]
    gain_slots = [part[:, qkv_width:] for part in packed_slots]
    (output_own,) = after((w_output,), qkv_ring[-1])
    output_ring = gather_ring(output_own, "z")
    output_ring_sent = after(output_ring, *packed_slots)
    output_slots = [gather_rows(part, k) for k, part in enumerate(output_ring_sent)]
    unit = jnp.eye(slot_rows, dtype=BF16)
    gain_one_rel = jnp.concatenate([tdot(part, unit)[:1] for part in gain_slots], axis=1)
    gain_twof = sum(
        lax.dot_general(
            part,
            selector[:, k * slot_rows : (k + 1) * slot_rows],
            (((0,), (1,)), ((), ())),
            preferred_element_type=F32,
        )[1]
        for k, part in enumerate(gain_slots)
    )

    ff_width = w_gate.shape[1]
    ff_own = ff_width // size_z
    ff_rows = w_gate.shape[0]
    w_down_t = w_down.T

    def hidden_block(which):
        start = which * ff_own
        return jnp.concatenate(
            [
                lax.dynamic_slice_in_dim(w_gate, start, ff_own, axis=1),
                lax.dynamic_slice_in_dim(w_up, start, ff_own, axis=1),
                lax.dynamic_slice_in_dim(w_down_t, start, ff_own, axis=1),
            ],
            axis=1,
        )

    blocks = [hidden_block(ahead(at_z, k, size_z)) for k in range(size_z)]
    blocks = after(blocks, output_ring[-1])
    blocks = [shift(b, "z", k) if k else b for k, b in enumerate(blocks)]
    xfloat = tokens.reshape(token_rows, width).astype(F32)
    inv_one = lax.rsqrt(jnp.mean(xfloat * xfloat, axis=-1, keepdims=True) + EPS_NORM)
    normed_one = by_distance(tokens.reshape(token_rows, width)).astype(F32) * inv_one
    hidden_by_distance = (normed_one * gain_one_rel).astype(BF16)
    qkv = rows_product(hidden_by_distance, qkv_slots)
    query_rows = qkv[:, :query_width].reshape(
        local_sequence, context_rows, QUERY_HEADS, HEAD_WIDTH
    )
    unrotated_key = qkv[:, query_width : query_width + kv_width].reshape(
        local_sequence, context_rows, KEY_VALUE_HEADS, HEAD_WIDTH
    )
    value_own = (
        qkv[:, query_width + kv_width :].astype(BF16).reshape(local_sequence, context_rows, kv_width)
    )
    cosine_table, sine_table = rope_tables(positions, HEAD_WIDTH // 2)
    rotated_query = (
        apply_rotation(query_rows, cosine_table, sine_table)
        .astype(BF16)
        .reshape(local_sequence, context_rows, KEY_VALUE_HEADS, query_groups, HEAD_WIDTH)
    )
    rkey_own = (
        apply_rotation(unrotated_key, cosine_table, sine_table)
        .astype(BF16)
        .reshape(local_sequence, context_rows, kv_width)
    )

    def gather_sequence(value):
        value = jnp.concatenate(gather_ring(value, "x"), axis=1)
        return jnp.concatenate(gather_ring(value, "c"), axis=1)

    at_ctx = at_x * size_c + at_c
    query_index = at_ctx * context_rows + jnp.arange(context_rows, dtype=jnp.int32)
    slot = jnp.arange(count_ctx, dtype=jnp.int32)
    slot_ctx = ((at_x - slot % size_x) % size_x) * size_c + (at_c - slot // size_x) % size_c
    key_index = (
        slot_ctx[:, None] * context_rows + jnp.arange(context_rows, dtype=jnp.int32)[None, :]
    ).reshape(-1)
    segments_all = gather_sequence(segment_ids)
    allowed = (segment_ids[:, :, None] == segments_all[:, None, :]) & (
        key_index[None, None, :] <= query_index[None, :, None]
    )
    allowed = allowed[:, None, None]
    gathered = gather_sequence(jnp.concatenate([rkey_own, value_own], axis=-1))
    ffn = jnp.zeros((width, 3 * ff_own), BF16)
    blocks = after(blocks, gathered)
    for step, block in enumerate(blocks):
        block_y = gather_ring(block, "y")
        for k, piece_y in enumerate(block_y):
            row = back(at_z, step, size_z) * size_y + back(at_y, k, size_y)
            ffn = lax.dynamic_update_slice_in_dim(ffn, piece_y, row * ff_rows, axis=0)
    gate_up_weight = ffn[:, : 2 * ff_own]
    down_weight_t = ffn[:, 2 * ff_own :]

    gathered_keys = gathered[..., :kv_width].reshape(
        local_sequence, sequence_length, KEY_VALUE_HEADS, HEAD_WIDTH
    )
    gathered_values = gathered[..., kv_width:].reshape(
        local_sequence, sequence_length, KEY_VALUE_HEADS, HEAD_WIDTH
    )
    scores = (
        jnp.einsum("schgd,slhd->shgcl", rotated_query, gathered_keys, preferred_element_type=F32)
        * factor
    )
    masked = jnp.where(allowed, scores, MASKED)
    expo = jnp.exp(masked)
    total = jnp.sum(expo, axis=-1, keepdims=True)
    lse = jnp.log(total)
    probs = (expo / total).astype(BF16)
    attended = jnp.einsum("shgcl,slhd->schgd", probs, gathered_values, preferred_element_type=F32)
    attended = attended.astype(BF16).reshape(token_rows, query_width)
    (cot_own,) = after((cotangent.reshape(token_rows, width),), attended)
    cot_slots = gather_tokens(cot_own)
    attended_by_distance = by_distance(attended)
    resid = xfloat + rows_product(attended_by_distance, output_slots)
    inv_two = lax.rsqrt(jnp.mean(resid * resid, axis=-1, keepdims=True) + EPS_NORM)
    normed_two = resid * inv_two
    h_two = (normed_two * gain_twof).astype(BF16)

    h_slots = gather_tokens(h_two)
    d_h_slots = []
    group_rows = token_rows * size_z * count_ctx
    hidden_all = jnp.zeros((group_rows, ff_own), BF16)
    d_gate_all = jnp.zeros((group_rows, ff_own), BF16)
    d_up_all = jnp.zeros((group_rows, ff_own), BF16)
    for h_slot, cot_slot in zip(h_slots, cot_slots):
        gate_up = jnp.dot(h_slot, gate_up_weight, preferred_element_type=F32)
        gate, up_proj = gate_up[:, :ff_own], gate_up[:, ff_own:]
        sigma = jax.nn.sigmoid(gate)
        hidden = (gate * sigma * up_proj).astype(BF16)
        d_hidden = jnp.dot(cot_slot, down_weight_t, preferred_element_type=F32)
        d_up = (d_hidden * gate * sigma).astype(BF16)
        d_gate = (d_hidden * up_proj * sigma * (1.0 + gate * (1.0 - sigma))).astype(BF16)
        d_both = jnp.concatenate([d_gate, d_up], axis=1)
        d_h_slots.append(dot_t(d_both, gate_up_weight).astype(BF16))
        at_row = len(d_h_slots) * hidden.shape[0] - hidden.shape[0]
        hidden_all = lax.dynamic_update_slice(hidden_all, hidden, (at_row, 0))
        d_gate_all = lax.dynamic_update_slice(d_gate_all, d_gate, (at_row, 0))
        d_up_all = lax.dynamic_update_slice(d_up_all, d_up, (at_row, 0))
    d_h_sum = reduce_ring(reduce_locally(d_h_slots), "z")
    h_all = jnp.concatenate(h_slots, axis=0)
    cot_all = jnp.concatenate(cot_slots, axis=0)
    grad_ffn = [
        tdot(h_all, d_gate_all).astype(BF16),
        tdot(h_all, d_up_all).astype(BF16),
        tdot(cot_all, hidden_all).astype(BF16),
    ]
    out = dot_t(hidden_all, down_weight_t).astype(BF16)
    (d_h_sum,), grad_ffn, out = lax.optimization_barrier(((d_h_sum,), grad_ffn, out))
    d_h_two = d_h_sum.astype(F32)

    out = out.reshape(size_z, -1, width)
    out_cores = reduce_axes(out, ("c",))
    pairs_y = []
    for k in range(size_y):
        rows_y = []
        for step in range(size_z):
            row = back(at_z, step, size_z) * size_y + back(at_y, k, size_y)
            rows_y.append(
                jnp.concatenate(
                    [
                        lax.dynamic_slice_in_dim(part, row * ff_rows, ff_rows, axis=0)
                        for part in grad_ffn
                    ],
                    axis=1,
                )
            )
        pairs_y.append(rows_y)
    ffn_own = [
        reduce_ring([pairs_y[k][step] for k in range(size_y)], "y") for step in range(size_z)
    ]

    gain_term_two = jnp.sum(d_h_two * normed_two, axis=0)
    cot_rows = cotangent.reshape(token_rows, width)
    d_resid = cot_rows.astype(F32) + norm_back(d_h_two, normed_two, inv_two, gain_twof)
    residual_gradient_second = d_resid.astype(BF16)
    (out_cores,) = after((out_cores,), residual_gradient_second)
    early = [k for k in range(size_z) if k in (1, 2)]
    late = [k for k in range(size_z) if k not in early]
    out_early = reduce_axes(jnp.stack([out_cores[k] for k in early]), ("x",))
    attended_gradient = by_feature(
        jnp.concatenate([dot_t(residual_gradient_second, part) for part in output_slots], axis=1)
    ).astype(BF16)
    attended_gradient = attended_gradient.reshape(
        local_sequence, context_rows, KEY_VALUE_HEADS, query_groups, HEAD_WIDTH
    )
    part = tdot(attended_by_distance, residual_gradient_second).astype(BF16)
    part_cores = reduce_axes(part.reshape(size_z, -1, width), ("c",))
    probs_f = jnp.where(allowed, jnp.exp(masked - lse), 0.0)
    d_probs = jnp.einsum(
        "schgd,slhd->shgcl", attended_gradient, gathered_values, preferred_element_type=F32
    )
    delta = jnp.sum(probs_f * d_probs, axis=-1, keepdims=True)
    d_scores_b = (probs_f * (d_probs - delta) * factor).astype(BF16)
    value_gradient_local = jnp.einsum(
        "shgcl,schgd->slhd",
        probs_f.astype(BF16),
        attended_gradient,
        preferred_element_type=F32,
    )
    d_rquery = jnp.einsum(
        "shgcl,slhd->schgd", d_scores_b, gathered_keys, preferred_element_type=F32
    )
    rotated_key_gradient = jnp.einsum(
        "shgcl,schgd->slhd", d_scores_b, rotated_query, preferred_element_type=F32
    )
    kv_gradient = jnp.concatenate(
        [
            rotated_key_gradient.reshape(local_sequence, sequence_length, kv_width).astype(BF16),
            value_gradient_local.reshape(local_sequence, sequence_length, kv_width).astype(BF16),
        ],
        axis=-1,
    )
    for axis in ("c", "x"):
        count = lax.axis_size(axis)
        kv_gradient = reduce_ring(jnp.split(kv_gradient, count, axis=1), axis)
    out_cores, part_cores = after((out_cores, part_cores), kv_gradient)
    out_late = reduce_axes(jnp.stack([out_cores[k] for k in late]), ("x",))
    out_across = {k: out_early[n] for n, k in enumerate(early)}
    out_across.update({k: out_late[n] for n, k in enumerate(late)})
    ffn_out = out_across[1]
    for k in range(2, size_z):
        ffn_out = add_rounded(shift(ffn_out, "z"), out_across[k])
    ffn_own = after(ffn_own, ffn_out)
    ffn_out = shift(ffn_out, "z")
    ffn_sums = [shift(b, "z", -step) if step else b for step, b in enumerate(ffn_own)]
    part_even = reduce_axes(part_cores[0::2], ("x", "y"))
    part_odd = reduce_axes(part_cores[1::2], ("y", "x"))
    dquery = (
        reverse_rotation(
            d_rquery.reshape(local_sequence, context_rows, QUERY_HEADS, HEAD_WIDTH),
            cosine_table,
            sine_table,
        )
        .astype(BF16)
        .reshape(token_rows, query_width)
    )
    dkey = (
        reverse_rotation(
            kv_gradient[..., :kv_width].reshape(
                local_sequence, context_rows, KEY_VALUE_HEADS, HEAD_WIDTH
            ),
            cosine_table,
            sine_table,
        )
        .astype(BF16)
        .reshape(token_rows, kv_width)
    )
    dvalue = kv_gradient[..., kv_width:].astype(BF16).reshape(token_rows, kv_width)
    d_qkv = jnp.concatenate([dquery, dkey, dvalue], axis=1)
    d_h_one = jnp.concatenate([dot_t(d_qkv, part) for part in qkv_slots], axis=1)
    gain_term_one = jnp.sum(d_h_one * normed_one, axis=0, keepdims=True)

    def split(row):
        high = row.astype(BF16)
        return jnp.concatenate([high, (row - high.astype(F32)).astype(BF16)], axis=0)

    gain_rows = jnp.concatenate(
        [
            split(gain_term_one),
            by_distance(split(gain_term_two[None])),
            jnp.zeros((4, width), BF16),
        ],
        axis=0,
    )
    which = jnp.arange(8, dtype=jnp.int32)[:, None] // 2
    gain_places = (which == jnp.arange(lanes, dtype=jnp.int32)[None, :]).astype(BF16)
    left = jnp.concatenate([hidden_by_distance, gain_rows], axis=0)
    right = jnp.concatenate(
        [
            jnp.concatenate([d_qkv, jnp.zeros((token_rows, lanes), BF16)], axis=1),
            jnp.concatenate([jnp.zeros((8, qkv_width), BF16), gain_places], axis=1),
        ],
        axis=0,
    )
    grad_qkv, local = reduce_weight(left, right)
    grad_qkv = grad_qkv.astype(F32)
    part_even, part_odd = after((part_even, part_odd), local[0])
    output_local = [(part_odd if k % 2 else part_even)[k // 2] for k in range(size_z)]
    grad_output = reduce_ring(output_local, "z").astype(F32)
    (ffn_out,) = after((ffn_out,), local[0])
    mixed = (resid + add_rounded(ffn_out, out_across[0]).astype(F32)).astype(BF16)
    ffn_sums = after(ffn_sums, local[0])
    grad_gate = jnp.zeros((ff_rows, ff_width), F32)
    grad_up = jnp.zeros((ff_rows, ff_width), F32)
    grad_down_t = jnp.zeros((ff_rows, ff_width), F32)
    for step, block in enumerate(ffn_sums):
        start = ahead(at_z, step, size_z) * ff_own
        block = block.astype(F32)
        grad_gate = lax.dynamic_update_slice_in_dim(grad_gate, block[:, :ff_own], start, axis=1)
        grad_up = lax.dynamic_update_slice_in_dim(
            grad_up, block[:, ff_own : 2 * ff_own], start, axis=1
        )
        grad_down_t = lax.dynamic_update_slice_in_dim(
            grad_down_t, block[:, 2 * ff_own :], start, axis=1
        )
    grad_down = grad_down_t.T
    grad_tokens = d_resid + by_feature(norm_back(d_h_one, normed_one, inv_one, gain_one_rel))
    return (
        mixed.reshape(local_sequence, context_rows, width),
        grad_tokens.reshape(local_sequence, context_rows, width),
        grad_qkv[:, qkv_width],
        grad_qkv[:, :query_width],
        grad_qkv[:, query_width : query_width + kv_width],
        grad_qkv[:, query_width + kv_width : qkv_width],
        grad_output,
        grad_qkv[:, qkv_width + 1],
        grad_gate,
        grad_up,
        grad_down,
    )


def solution(mesh):
    count_dp, count_ctx = mesh.devices.shape
    along_z = 4 if count_dp % 4 == 0 else count_dp
    along_x = 2 if count_ctx % 2 == 0 else 1
    fine = Mesh(
        mesh.devices.reshape(along_z, count_dp // along_z, along_x, count_ctx // along_x),
        ("z", "y", "x", "c"),
    )
    dp, ctx, both = ("z", "y"), ("x", "c"), ("z", "y", "x", "c")
    return jax.shard_map(
        layer,
        mesh=fine,
        in_specs=(
            P(dp, ctx, None),
            P(dp, ctx),
            P(dp, ctx),
            P(both),
            P(both, None),
            P(both, None),
            P(both, None),
            P(both, None),
            P(both),
            P(dp, ctx),
            P(dp, ctx),
            P(ctx, dp),
            P(dp, ctx, None),
        ),
        out_specs=(
            P(dp, ctx, None),
            P(dp, ctx, None),
            P(both),
            P(both, None),
            P(both, None),
            P(both, None),
            P(both, None),
            P(both),
            P(dp, ctx),
            P(dp, ctx),
            P(ctx, dp),
        ),
        check_vma=False,
    )
```

profile of v0, /device:TPU:0, one launch (start us, length us, event | category | flops | bytes accessed | tf_op | source)
XLA Modules:
  0.0 874.2 jit_solution(812688873035791388)
XLA Ops:
  13.3 5.7 iota_compare_fusion
  41.3 25.5 %collective-permute-done.4 = bf16[64,3200]{1,0:T(8,128)(2,1)S(1)} collective-permute-done((bf16[64,3200]{1,0:T(8,128)(2,1)S(1)}, bf16[64,3200]{1,0:T(8,128)(2,1)S(1)}, u32[]{:S(2)}, u32[]{:S(2)}) %collective-permute-start.4) | collective-permute-done | bytes 409632 | tf_op jit(solution)/shard_map/ppermute | solution.py:79
  70.6 9.0 %collective-permute-done.11 = bf16[64,3200]{1,0:T(8,128)(2,1)S(1)} collective-permute-done((bf16[64,3200]{1,0:T(8,128)(2,1)S(1)}, bf16[64,3200]{1,0:T(8,128)(2,1)S(1)}, u32[]{:S(2)}, u32[]{:S(2)}) %collective-permute-start.11) | collective-permute-done | bytes 409632 | tf_op jit(solution)/shard_map/ppermute | solution.py:79
  79.8 15.3 %collective-permute-done.8 = bf16[64,3200]{1,0:T(8,128)(2,1)S(1)} collective-permute-done((bf16[64,3200]{1,0:T(8,128)(2,1)S(1)}, bf16[64,3200]{1,0:T(8,128)(2,1)S(1)}, u32[]{:S(2)}, u32[]{:S(2)}) %collective-permute-start.8) | collective-permute-done | bytes 409632 | tf_op jit(solution)/shard_map/ppermute | solution.py:79
  99.2 23.4 %collective-permute-done.12 = bf16[64,3200]{1,0:T(8,128)(2,1)S(1)} collective-permute-done((bf16[64,3200]{1,0:T(8,128)(2,1)S(1)}, bf16[64,3200]{1,0:T(8,128)(2,1)S(1)}, u32[]{:S(2)}, u32[]{:S(2)}) %collective-permute-start.12) | collective-permute-done | bytes 409632 | tf_op jit(solution)/shard_map/ppermute | solution.py:79
  125.0 6.9 collective-permute-done.21
  133.9 6.7 collective-permute-done.13
  151.1 4.2 multiply_convert_fusion.14
  230.1 5.4 collective-permute-done.68
  241.6 14.5 %collective-permute-done.41 = bf16[256,1536]{0,1:T(8,128)(2,1)S(1)} collective-permute-done((bf16[256,1536]{0,1:T(8,128)(2,1)}, bf16[256,1536]{0,1:T(8,128)(2,1)S(1)}, u32[]{:S(2)}, u32[]{:S(2)}) %collective-permute-start.41) | collective-permute-done | bytes 786464 | tf_op jit(solution)/shard_map/ppermute | solution.py:79
  258.6 14.4 %collective-permute-done.42 = bf16[256,1536]{0,1:T(8,128)(2,1)S(1)} collective-permute-done((bf16[256,1536]{0,1:T(8,128)(2,1)}, bf16[256,1536]{0,1:T(8,128)(2,1)S(1)}, u32[]{:S(2)}, u32[]{:S(2)}) %collective-permute-start.42) | collective-permute-done | bytes 786464 | tf_op jit(solution)/shard_map/ppermute | solution.py:79
  275.8 12.8 %collective-permute-done.43 = bf16[256,1536]{0,1:T(8,128)(2,1)S(1)} collective-permute-done((bf16[256,1536]{0,1:T(8,128)(2,1)}, bf16[256,1536]{0,1:T(8,128)(2,1)S(1)}, u32[]{:S(2)}, u32[]{:S(2)}) %collective-permute-start.43) | collective-permute-done | bytes 786464 | tf_op jit(solution)/shard_map/ppermute | solution.py:79
  289.7 13.6 %collective-permute-done.50 = bf16[128,2048]{1,0:T(8,128)(2,1)S(1)} collective-permute-done((bf16[128,2048]{1,0:T(8,128)(2,1)S(1)}, bf16[128,2048]{1,0:T(8,128)(2,1)S(1)}, u32[]{:S(2)}, u32[]{:S(2)}) %collective-permute-start.50) | collective-permute-done | bytes 524320 | tf_op jit(solution)/shard_map/ppermute | solution.py:79
  313.9 4.2 collective-permute-done.51
  324.1 5.2 collective-permute-done.70
  335.6 5.0 collective-permute-done.60
  343.5 8.0 collective-permute-done.45
  374.3 3.7 fusion.72
  410.9 9.6 %convolution_convert_fusion.12 = bf16[2048,512]{1,0:T(8,128)(2,1)} fusion(bf16[2048,2048]{1,0:T(8,128)(2,1)} %constant_dynamic-update-slice_fusion.28, bf16[2048,512]{0,1:T(8,128)(2,1)S(1)} %get-tuple-element.113), kind=kOutput, calls=%fused_computation.57 | convolution fusion | flops 4296015872 | bytes 12582912 | tf_op jit(solution)/shard_map/dot_general | solution.py:58
  422.9 9.5 %convolution_convert_fusion.11 = bf16[2048,512]{1,0:T(8,128)(2,1)} fusion(bf16[2048,2048]{1,0:T(8,128)(2,1)} %constant_dynamic-update-slice_fusion.28, bf16[2048,512]{0,1:T(8,128)(2,1)S(1)} %get-tuple-element.125), kind=kOutput, calls=%fused_computation.56 | convolution fusion | flops 4296015872 | bytes 12582912 | tf_op jit(solution)/shard_map/dot_general | solution.py:58
  432.4 4.5 collective-permute-done.49
  439.4 9.5 %convolution_convert_fusion.10 = bf16[2048,512]{1,0:T(8,128)(2,1)} fusion(bf16[2048,2048]{1,0:T(8,128)(2,1)} %constant_dynamic-update-slice_fusion.40, bf16[2048,512]{0,1:T(8,128)(2,1)S(1)} %get-tuple-element.157), kind=kOutput, calls=%fused_computation.55 | convolution fusion | flops 4296015872 | bytes 12582912 | tf_op jit(solution)/shard_map/dot_general | solution.py:58
  448.9 3.7 collective-permute-done.58
  454.0 6.8 convolution_convert_fusion
  460.8 6.7 collective-permute-done.67
  469.6 5.6 convolution_convert_fusion.1
  485.7 5.5 fusion.5
  491.3 5.4 fusion.121
  496.7 5.5 fusion.14
  525.8 5.3 collective-permute-done.80
  555.2 14.6 %collective-permute-done.107 = bf16[256,1536]{1,0:T(8,128)(2,1)} collective-permute-done((bf16[256,1536]{1,0:T(8,128)(2,1)}, bf16[256,1536]{1,0:T(8,128)(2,1)}, u32[]{:S(2)}, u32[]{:S(2)}) %collective-permute-start.107) | collective-permute-done | bytes 786464 | tf_op jit(solution)/shard_map/ppermute | solution.py:79
  574.5 11.3 %collective-permute-done.108 = bf16[256,1536]{1,0:T(8,128)(2,1)S(1)} collective-permute-done((bf16[256,1536]{1,0:T(8,128)(2,1)S(1)}, bf16[256,1536]{1,0:T(8,128)(2,1)S(1)}, u32[]{:S(2)}, u32[]{:S(2)}) %collective-permute-start.108) | collective-permute-done | bytes 786464 | tf_op jit(solution)/shard_map/ppermute | solution.py:79
  588.8 5.0 fusion.49
  600.1 15.8 %collective-permute-done.87 = bf16[128,3200]{1,0:T(8,128)(2,1)S(1)} collective-permute-done((bf16[128,3200]{1,0:T(8,128)(2,1)S(1)}, bf16[128,3200]{1,0:T(8,128)(2,1)S(1)}, u32[]{:S(2)}, u32[]{:S(2)}) %collective-permute-start.87) | collective-permute-done | bytes 819232 | tf_op jit(solution)/shard_map/ppermute | solution.py:79
  619.1 13.4 %collective-permute-done.95 = bf16[128,3200]{1,0:T(8,128)(2,1)S(1)} collective-permute-done((bf16[128,3200]{1,0:T(8,128)(2,1)S(1)}, bf16[128,3200]{1,0:T(8,128)(2,1)S(1)}, u32[]{:S(2)}, u32[]{:S(2)}) %collective-permute-start.95) | collective-permute-done | bytes 819232 | tf_op jit(solution)/shard_map/ppermute | solution.py:79
  634.5 8.8 %collective-permute-done.88 = bf16[64,3200]{1,0:T(8,128)(2,1)S(1)} collective-permute-done((bf16[64,3200]{1,0:T(8,128)(2,1)S(1)}, bf16[64,3200]{1,0:T(8,128)(2,1)S(1)}, u32[]{:S(2)}, u32[]{:S(2)}) %collective-permute-start.88) | collective-permute-done | bytes 409632 | tf_op jit(solution)/shard_map/ppermute | solution.py:79
  646.9 8.7 collective-permute-done.89
  656.5 5.5 add_convert_fusion.1
  663.6 4.1 add_convert_fusion
  672.4 7.2 collective-permute-done.97
  681.4 49.0 %collective-permute-done.98 = bf16[2,128,2048]{2,1,0:T(8,128)(2,1)S(1)} collective-permute-done((bf16[2,128,2048]{2,1,0:T(8,128)(2,1)S(1)}, bf16[2,128,2048]{2,1,0:T(8,128)(2,1)S(1)}, u32[]{:S(2)}, u32[]{:S(2)}) %collective-permute-start.98) | collective-permute-done | bytes 1048608 | tf_op jit(solution)/shard_map/ppermute | solution.py:79
  733.8 6.4 collective-permute-done.99
  741.2 7.8 collective-permute-done.76
  749.2 5.4 collective-permute-done.102
  755.2 12.0 %collective-permute-done.103 = bf16[64,2048]{1,0:T(8,128)(2,1)S(1)} collective-permute-done((bf16[64,2048]{1,0:T(8,128)(2,1)S(1)}, bf16[64,2048]{1,0:T(8,128)(2,1)S(1)}, u32[]{:S(2)}, u32[]{:S(2)}) %collective-permute-start.103) | collective-permute-done | bytes 262176 | tf_op jit(solution)/shard_map/ppermute | solution.py:79
  779.3 10.3 %collective-permute-done.82 = bf16[128,2048]{1,0:T(8,128)(2,1)S(1)} collective-permute-done((bf16[128,2048]{1,0:T(8,128)(2,1)S(1)}, bf16[128,2048]{1,0:T(8,128)(2,1)S(1)}, u32[]{:S(2)}, u32[]{:S(2)}) %collective-permute-start.82) | collective-permute-done | bytes 524320 | tf_op jit(solution)/shard_map/ppermute | solution.py:79
  790.7 11.5 %collective-permute-done.109 = bf16[256,1536]{1,0:T(8,128)(2,1)S(1)} collective-permute-done((bf16[256,1536]{1,0:T(8,128)(2,1)S(1)}, bf16[256,1536]{1,0:T(8,128)(2,1)S(1)}, u32[]{:S(2)}, u32[]{:S(2)}) %collective-permute-start.109) | collective-permute-done | bytes 786464 | tf_op jit(solution)/shard_map/ppermute | solution.py:79
  802.2 49.7 %collective-permute-done.110 = bf16[256,1536]{1,0:T(8,128)(2,1)S(1)} collective-permute-done((bf16[256,1536]{1,0:T(8,128)(2,1)S(1)}, bf16[256,1536]{1,0:T(8,128)(2,1)S(1)}, u32[]{:S(2)}, u32[]{:S(2)}) %collective-permute-start.110) | collective-permute-done | bytes 786464 | tf_op jit(solution)/shard_map/ppermute | solution.py:79
  (760 shorter events, 362.9 us)
Async XLA Ops:
  3.3 34.9 %collective-permute-start.3 = (bf16[64,3200]{1,0:T(8,128)(2,1)}, bf16[64,3200]{1,0:T(8,128)(2,1)S(1)}, u32[]{:S(2)}, u32[]{:S(2)}) collective-permute-start(bf16[64,3200]{1,0:T(8,128)(2,1)} %pad_maximum_fusion.42), channel_id=1, source_target_pairs={{0,8},{8,16},{16,24},{24,0},{1,9},{9,17},{17,25},{25,1},{2,10},{10... | collective-permute-start | bytes 1228808 | tf_op jit(solution)/shard_map/ppermute | solution.py:79
  6.3 31.2 %collective-permute-start = (bf16[64,3200]{1,0:T(8,128)(2,1)}, bf16[64,3200]{1,0:T(8,128)(2,1)S(1)}, u32[]{:S(2)}, u32[]{:S(2)}) collective-permute-start(bf16[64,3200]{1,0:T(8,128)(2,1)} %pad_maximum_fusion.42), channel_id=1, source_target_pairs={{0,4},{4,0},{1,5},{5,1},{2,6},{6,2},{3,7},{7,3},{8,12},{12,8},{9,1... | collective-permute-start | bytes 1228808 | tf_op jit(solution)/shard_map/ppermute | solution.py:79
  7.8 26.4 %collective-permute-start.17 = (s32[1,128]{1,0:T(1,128)}, s32[1,128]{1,0:T(1,128)}, u32[]{:S(2)}, u32[]{:S(2)}) collective-permute-start(s32[1,128]{1,0:T(1,128)} %param.14), channel_id=1, source_target_pairs={{0,2},{2,0},{1,3},{3,1},{4,6},{6,4},{5,7},{7,5},{8,10},{10,8},{9,1... | collective-permute-start | bytes 1544 | tf_op jit(solution)/shard_map/ppermute | solution.py:79
  37.6 42.0 %collective-permute-start.1 = (bf16[128,3200]{1,0:T(8,128)(2,1)S(1)}, bf16[128,3200]{1,0:T(8,128)(2,1)S(1)}, u32[]{:S(2)}, u32[]{:S(2)}) collective-permute-start(bf16[128,3200]{1,0:T(8,128)(2,1)S(1)} %pad_maximum_fusion.21), channel_id=1, source_target_pairs={{0,2},{2,0},{1,3},{3,1},{4,6},{6,4},{5,7},{7,5},{8,10},{10,8},{9,1... | collective-permute-start | bytes 2457608 | tf_op jit(solution)/shard_map/ppermute | solution.py:79
  38.2 29.2 %collective-permute-start.7 = (bf16[64,3200]{1,0:T(8,128)(2,1)S(1)}, bf16[64,3200]{1,0:T(8,128)(2,1)S(1)}, u32[]{:S(2)}, u32[]{:S(2)}) collective-permute-start(bf16[64,3200]{1,0:T(8,128)(2,1)S(1)} %collective-permute-done.3), channel_id=1, source_target_pairs={{0,8},{8,16},{16,24},{24,0},{1,9},{9,17},{17,25},{25,1},{2,10},{10... | collective-permute-start | bytes 1228808 | tf_op jit(solution)/shard_map/ppermute | solution.py:79
  39.8 27.0 %collective-permute-start.4 = (bf16[64,3200]{1,0:T(8,128)(2,1)S(1)}, bf16[64,3200]{1,0:T(8,128)(2,1)S(1)}, u32[]{:S(2)}, u32[]{:S(2)}) collective-permute-start(bf16[64,3200]{1,0:T(8,128)(2,1)S(1)} %collective-permute-done.3), channel_id=1, source_target_pairs={{0,2},{2,0},{1,3},{3,1},{4,6},{6,4},{5,7},{7,5},{8,10},{10,8},{9,1... | collective-permute-start | bytes 1228808 | tf_op jit(solution)/shard_map/ppermute | solution.py:79
  66.8 32.2 %collective-permute-start.5 = (bf16[128,3200]{1,0:T(8,128)(2,1)S(1)}, bf16[128,3200]{1,0:T(8,128)(2,1)S(1)}, u32[]{:S(2)}, u32[]{:S(2)}) collective-permute-start(bf16[128,3200]{1,0:T(8,128)(2,1)S(1)} %pad_maximum_fusion.22), channel_id=1, source_target_pairs={{0,4},{4,0},{1,5},{5,1},{2,6},{6,2},{3,7},{7,3},{8,12},{12,8},{9,1... | collective-permute-start | bytes 2457608 | tf_op jit(solution)/shard_map/ppermute | solution.py:79
  69.0 26.1 %collective-permute-start.8 = (bf16[64,3200]{1,0:T(8,128)(2,1)S(1)}, bf16[64,3200]{1,0:T(8,128)(2,1)S(1)}, u32[]{:S(2)}, u32[]{:S(2)}) collective-permute-start(bf16[64,3200]{1,0:T(8,128)(2,1)S(1)} %collective-permute-done.7), channel_id=1, source_target_pairs={{0,4},{4,0},{1,5},{5,1},{2,6},{6,2},{3,7},{7,3},{8,12},{12,8},{9,1... | collective-permute-start | bytes 1228808 | tf_op jit(solution)/shard_map/ppermute | solution.py:79
  79.7 63.2 %collective-permute-start.2 = (bf16[256,3200]{1,0:T(8,128)(2,1)S(1)}, bf16[256,3200]{1,0:T(8,128)(2,1)S(1)}, u32[]{:S(2)}, u32[]{:S(2)}) collective-permute-start(bf16[256,3200]{1,0:T(8,128)(2,1)S(1)} %pad_maximum_fusion.1), channel_id=1, source_target_pairs={{0,1},{1,0},{2,3},{3,2},{4,5},{5,4},{6,7},{7,6},{8,9},{9,8},{10,11... | collective-permute-start | bytes 4915208 | tf_op jit(solution)/shard_map/ppermute | solution.py:79
  95.2 36.9 %collective-permute-start.9 = (bf16[128,3200]{1,0:T(8,128)(2,1)S(1)}, bf16[128,3200]{1,0:T(8,128)(2,1)S(1)}, u32[]{:S(2)}, u32[]{:S(2)}) collective-permute-start(bf16[128,3200]{1,0:T(8,128)(2,1)S(1)} %pad_maximum_fusion.23), channel_id=1, source_target_pairs={{0,2},{2,0},{1,3},{3,1},{4,6},{6,4},{5,7},{7,5},{8,10},{10,8},{9,1... | collective-permute-start | bytes 2457608 | tf_op jit(solution)/shard_map/ppermute | solution.py:79
  95.8 26.8 %collective-permute-start.12 = (bf16[64,3200]{1,0:T(8,128)(2,1)S(1)}, bf16[64,3200]{1,0:T(8,128)(2,1)S(1)}, u32[]{:S(2)}, u32[]{:S(2)}) collective-permute-start(bf16[64,3200]{1,0:T(8,128)(2,1)S(1)} %collective-permute-done.11), channel_id=1, source_target_pairs={{0,2},{2,0},{1,3},{3,1},{4,6},{6,4},{5,7},{7,5},{8,10},{10,8},{9,1... | collective-permute-start | bytes 1228808 | tf_op jit(solution)/shard_map/ppermute | solution.py:79
  97.4 26.0 %collective-permute-start.20 = (bf16[64,2048]{1,0:T(8,128)(2,1)S(1)}, bf16[64,2048]{1,0:T(8,128)(2,1)}, u32[]{:S(2)}, u32[]{:S(2)}) collective-permute-start(bf16[64,2048]{1,0:T(8,128)(2,1)S(1)} %collective-permute-done.19), channel_id=1, source_target_pairs={{0,8},{8,16},{16,24},{24,0},{1,9},{9,17},{17,25},{25,1},{2,10},{10... | collective-permute-start | bytes 786440 | tf_op jit(solution)/shard_map/ppermute | solution.py:79
  99.1 46.6 %collective-permute-start.6 = (bf16[256,3200]{1,0:T(8,128)(2,1)S(1)}, bf16[256,3200]{1,0:T(8,128)(2,1)S(1)}, u32[]{:S(2)}, u32[]{:S(2)}) collective-permute-start(bf16[256,3200]{1,0:T(8,128)(2,1)S(1)} %pad_maximum_fusion.2), channel_id=1, source_target_pairs={{0,1},{1,0},{2,3},{3,2},{4,5},{5,4},{6,7},{7,6},{8,9},{9,8},{10,11... | collective-permute-start | bytes 4915208 | tf_op jit(solution)/shard_map/ppermute | solution.py:79
  131.9 71.6 %collective-permute-start.37 = (bf16[256,1536]{0,1:T(8,128)(2,1)}, bf16[256,1536]{0,1:T(8,128)(2,1)}, u32[]{:S(2)}, u32[]{:S(2)}) collective-permute-start(bf16[256,1536]{0,1:T(8,128)(2,1)} %pad_maximum_fusion.26), channel_id=1, source_target_pairs={{0,8},{8,16},{16,24},{24,0},{1,9},{9,17},{17,25},{25,1},{2,10},{10... | collective-permute-start | bytes 2359304 | tf_op jit(solution)/shard_map/ppermute | solution.py:79
  132.1 71.9 %collective-permute-start.38 = (bf16[256,1536]{0,1:T(8,128)(2,1)}, bf16[256,1536]{0,1:T(8,128)(2,1)}, u32[]{:S(2)}, u32[]{:S(2)}) collective-permute-start(bf16[256,1536]{0,1:T(8,128)(2,1)} %pad_maximum_fusion.27), channel_id=1, source_target_pairs={{0,16},{8,24},{16,0},{24,8},{1,17},{9,25},{17,1},{25,9},{2,18},{10... | collective-permute-start | bytes 2359304 | tf_op jit(solution)/shard_map/ppermute | solution.py:79
  140.5 63.9 %collective-permute-start.39 = (bf16[256,1536]{0,1:T(8,128)(2,1)}, bf16[256,1536]{0,1:T(8,128)(2,1)}, u32[]{:S(2)}, u32[]{:S(2)}) collective-permute-start(bf16[256,1536]{0,1:T(8,128)(2,1)} %pad_maximum_fusion.28), channel_id=1, source_target_pairs={{0,24},{8,0},{16,8},{24,16},{1,25},{9,1},{17,9},{25,17},{2,26},{10... | collective-permute-start | bytes 2359304 | tf_op jit(solution)/shard_map/ppermute | solution.py:79
  204.4 34.2 %collective-permute-start.40 = (bf16[256,1536]{0,1:T(8,128)(2,1)}, bf16[256,1536]{0,1:T(8,128)(2,1)S(1)}, u32[]{:S(2)}, u32[]{:S(2)}) collective-permute-start(bf16[256,1536]{0,1:T(8,128)(2,1)} %pad_maximum_fusion.25), channel_id=1, source_target_pairs={{0,4},{4,0},{1,5},{5,1},{2,6},{6,2},{3,7},{7,3},{8,12},{12,8},{9,1... | collective-permute-start | bytes 2359304 | tf_op jit(solution)/shard_map/ppermute | solution.py:79
  219.1 39.4 %collective-permute-start.34 = (bf16[128,2048]{1,0:T(8,128)(2,1)S(1)}, bf16[128,2048]{1,0:T(8,128)(2,1)S(1)}, u32[]{:S(2)}, u32[]{:S(2)}) collective-permute-start(bf16[128,2048]{1,0:T(8,128)(2,1)S(1)} %bitcast.223), channel_id=1, source_target_pairs={{0,8},{8,16},{16,24},{24,0},{1,9},{9,17},{17,25},{25,1},{2,10},{10... | collective-permute-start | bytes 1572872 | tf_op jit(solution)/shard_map/ppermute | solution.py:79
  221.7 67.3 %collective-permute-start.33 = (bf16[256,2048]{1,0:T(8,128)(2,1)S(1)}, bf16[256,2048]{1,0:T(8,128)(2,1)S(1)}, u32[]{:S(2)}, u32[]{:S(2)}) collective-permute-start(bf16[256,2048]{1,0:T(8,128)(2,1)S(1)} %pad_maximum_fusion.11), channel_id=1, source_target_pairs={{0,1},{1,0},{2,3},{3,2},{4,5},{5,4},{6,7},{7,6},{8,9},{9,8},{10,11... | collective-permute-start | bytes 3145736 | tf_op jit(solution)/shard_map/ppermute | solution.py:79
  225.0 78.3 %collective-permute-start.30 = (bf16[256,2048]{1,0:T(8,128)(2,1)S(1)}, bf16[256,2048]{1,0:T(8,128)(2,1)S(1)}, u32[]{:S(2)}, u32[]{:S(2)}) collective-permute-start(bf16[256,2048]{1,0:T(8,128)(2,1)S(1)} %pad_maximum_fusion.10), channel_id=1, source_target_pairs={{0,1},{1,0},{2,3},{3,2},{4,5},{5,4},{6,7},{7,6},{8,9},{9,8},{10,11... | collective-permute-start | bytes 3145736 | tf_op jit(solution)/shard_map/ppermute | solution.py:79
  238.5 34.4 %collective-permute-start.42 = (bf16[256,1536]{0,1:T(8,128)(2,1)}, bf16[256,1536]{0,1:T(8,128)(2,1)S(1)}, u32[]{:S(2)}, u32[]{:S(2)}) collective-permute-start(bf16[256,1536]{0,1:T(8,128)(2,1)} %collective-permute-done.38), channel_id=1, source_target_pairs={{0,4},{4,0},{1,5},{5,1},{2,6},{6,2},{3,7},{7,3},{8,12},{12,8},{9,1... | collective-permute-start | bytes 2359304 | tf_op jit(solution)/shard_map/ppermute | solution.py:79
  256.1 32.6 %collective-permute-start.43 = (bf16[256,1536]{0,1:T(8,128)(2,1)}, bf16[256,1536]{0,1:T(8,128)(2,1)S(1)}, u32[]{:S(2)}, u32[]{:S(2)}) collective-permute-start(bf16[256,1536]{0,1:T(8,128)(2,1)} %collective-permute-done.39), channel_id=1, source_target_pairs={{0,4},{4,0},{1,5},{5,1},{2,6},{6,2},{3,7},{7,3},{8,12},{12,8},{9,1... | collective-permute-start | bytes 2359304 | tf_op jit(solution)/shard_map/ppermute | solution.py:79
  258.5 46.7 %collective-permute-start.27 = (bf16[256,2048]{1,0:T(8,128)(2,1)S(1)}, bf16[256,2048]{1,0:T(8,128)(2,1)S(1)}, u32[]{:S(2)}, u32[]{:S(2)}) collective-permute-start(bf16[256,2048]{1,0:T(8,128)(2,1)S(1)} %pad_maximum_fusion.9), channel_id=1, source_target_pairs={{0,1},{1,0},{2,3},{3,2},{4,5},{5,4},{6,7},{7,6},{8,9},{9,8},{10,11... | collective-permute-start | bytes 3145736 | tf_op jit(solution)/shard_map/ppermute | solution.py:79
  289.1 29.1 %collective-permute-start.69 = (bf16[256,2048]{1,0:T(8,128)(2,1)S(1)}, bf16[256,2048]{1,0:T(8,128)(2,1)S(1)}, u32[]{:S(2)}, u32[]{:S(2)}) collective-permute-start(bf16[256,2048]{1,0:T(8,128)(2,1)S(1)} %pad_maximum_fusion.18), channel_id=1, source_target_pairs={{0,1},{1,0},{2,3},{3,2},{4,5},{5,4},{6,7},{7,6},{8,9},{9,8},{10,11... | collective-permute-start | bytes 3145736 | tf_op jit(solution)/shard_map/ppermute | solution.py:79
  303.3 37.4 %collective-permute-start.36 = (bf16[256,2048]{1,0:T(8,128)(2,1)S(1)}, bf16[256,2048]{1,0:T(8,128)(2,1)S(1)}, u32[]{:S(2)}, u32[]{:S(2)}) collective-permute-start(bf16[256,2048]{1,0:T(8,128)(2,1)S(1)} %pad_maximum_fusion.12), channel_id=1, source_target_pairs={{0,1},{1,0},{2,3},{3,2},{4,5},{5,4},{6,7},{7,6},{8,9},{9,8},{10,11... | collective-permute-start | bytes 3145736 | tf_op jit(solution)/shard_map/ppermute | solution.py:79
  318.2 39.0 %collective-permute-start.52 = (bf16[256,2048]{1,0:T(8,128)(2,1)S(1)}, bf16[256,2048]{1,0:T(8,128)(2,1)S(1)}, u32[]{:S(2)}, u32[]{:S(2)}) collective-permute-start(bf16[256,2048]{1,0:T(8,128)(2,1)S(1)} %pad_maximum_fusion.14), channel_id=1, source_target_pairs={{0,1},{1,0},{2,3},{3,2},{4,5},{5,4},{6,7},{7,6},{8,9},{9,8},{10,11... | collective-permute-start | bytes 3145736 | tf_op jit(solution)/shard_map/ppermute | solution.py:79
  329.4 30.7 %collective-permute-start.71 = (bf16[256,2048]{1,0:T(8,128)(2,1)S(1)}, bf16[256,2048]{1,0:T(8,128)(2,1)S(1)}, u32[]{:S(2)}, u32[]{:S(2)}) collective-permute-start(bf16[256,2048]{1,0:T(8,128)(2,1)S(1)} %pad_maximum_fusion.19), channel_id=1, source_target_pairs={{0,1},{1,0},{2,3},{3,2},{4,5},{5,4},{6,7},{7,6},{8,9},{9,8},{10,11... | collective-permute-start | bytes 3145736 | tf_op jit(solution)/shard_map/ppermute | solution.py:79
  340.7 32.6 %collective-permute-start.61 = (bf16[256,2048]{1,0:T(8,128)(2,1)S(1)}, bf16[256,2048]{1,0:T(8,128)(2,1)S(1)}, u32[]{:S(2)}, u32[]{:S(2)}) collective-permute-start(bf16[256,2048]{1,0:T(8,128)(2,1)S(1)} %pad_maximum_fusion.16), channel_id=1, source_target_pairs={{0,1},{1,0},{2,3},{3,2},{4,5},{5,4},{6,7},{7,6},{8,9},{9,8},{10,11... | collective-permute-start | bytes 3145736 | tf_op jit(solution)/shard_map/ppermute | solution.py:79
  390.6 70.3 %collective-permute-start.73 = (bf16[128,2048]{1,0:T(8,128)(2,1)}, bf16[128,2048]{1,0:T(8,128)(2,1)}, u32[]{:S(2)}, u32[]{:S(2)}) collective-permute-start(bf16[128,2048]{1,0:T(8,128)(2,1)} %slice.655), channel_id=1, source_target_pairs={{0,2},{2,0},{1,3},{3,1},{4,6},{6,4},{5,7},{7,5},{8,10},{10,8},{9,1... | collective-permute-start | bytes 1572872 | tf_op jit(solution)/shard_map/ppermute | solution.py:79
  409.6 27.6 %collective-permute-start.65 = (bf16[256,2048]{1,0:T(8,128)(2,1)S(1)}, bf16[256,2048]{1,0:T(8,128)(2,1)S(1)}, u32[]{:S(2)}, u32[]{:S(2)}) collective-permute-start(bf16[256,2048]{1,0:T(8,128)(2,1)S(1)} %slice.647), channel_id=1, source_target_pairs={{0,1},{1,0},{2,3},{3,2},{4,5},{5,4},{6,7},{7,6},{8,9},{9,8},{10,11... | collective-permute-start | bytes 3145736 | tf_op jit(solution)/shard_map/ppermute | solution.py:79
  507.0 149.4 %collective-permute-start.74 = (bf16[4,256,2048]{2,1,0:T(8,128)(2,1)}, bf16[4,256,2048]{2,1,0:T(8,128)(2,1)}, u32[]{:S(2)}, u32[]{:S(2)}) collective-permute-start(bf16[4,256,2048]{2,1,0:T(8,128)(2,1)} %slice.657), channel_id=1, source_target_pairs={{0,1},{1,0},{2,3},{3,2},{4,5},{5,4},{6,7},{7,6},{8,9},{9,8},{10,11... | collective-permute-start | bytes 12582920 | tf_op jit(solution)/shard_map/ppermute | solution.py:79
  509.4 154.2 %collective-permute-start.78 = (bf16[4,256,2048]{2,1,0:T(8,128)(2,1)}, bf16[4,256,2048]{2,1,0:T(8,128)(2,1)}, u32[]{:S(2)}, u32[]{:S(2)}) collective-permute-start(bf16[4,256,2048]{2,1,0:T(8,128)(2,1)} %slice.661), channel_id=1, source_target_pairs={{0,1},{1,0},{2,3},{3,2},{4,5},{5,4},{6,7},{7,6},{8,9},{9,8},{10,11... | collective-permute-start | bytes 12582920 | tf_op jit(solution)/shard_map/ppermute | solution.py:79
  515.3 34.5 %collective-permute-start.105 = (bf16[256,1536]{1,0:T(8,128)(2,1)}, bf16[256,1536]{1,0:T(8,128)(2,1)}, u32[]{:S(2)}, u32[]{:S(2)}) collective-permute-start(bf16[256,1536]{1,0:T(8,128)(2,1)} %pad_maximum_fusion.30), channel_id=1, source_target_pairs={{0,4},{4,0},{1,5},{5,1},{2,6},{6,2},{3,7},{7,3},{8,12},{12,8},{9,1... | collective-permute-start | bytes 2359304 | tf_op jit(solution)/shard_map/ppermute | solution.py:79
  518.4 34.6 %collective-permute-start.106 = (bf16[256,1536]{1,0:T(8,128)(2,1)}, bf16[256,1536]{1,0:T(8,128)(2,1)}, u32[]{:S(2)}, u32[]{:S(2)}) collective-permute-start(bf16[256,1536]{1,0:T(8,128)(2,1)} %pad_maximum_fusion.31), channel_id=1, source_target_pairs={{0,4},{4,0},{1,5},{5,1},{2,6},{6,2},{3,7},{7,3},{8,12},{12,8},{9,1... | collective-permute-start | bytes 2359304 | tf_op jit(solution)/shard_map/ppermute | solution.py:79
  531.1 38.7 %collective-permute-start.107 = (bf16[256,1536]{1,0:T(8,128)(2,1)}, bf16[256,1536]{1,0:T(8,128)(2,1)}, u32[]{:S(2)}, u32[]{:S(2)}) collective-permute-start(bf16[256,1536]{1,0:T(8,128)(2,1)} %pad_maximum_fusion.32), channel_id=1, source_target_pairs={{0,4},{4,0},{1,5},{5,1},{2,6},{6,2},{3,7},{7,3},{8,12},{12,8},{9,1... | collective-permute-start | bytes 2359304 | tf_op jit(solution)/shard_map/ppermute | solution.py:79
  550.7 35.1 %collective-permute-start.108 = (bf16[256,1536]{1,0:T(8,128)(2,1)S(1)}, bf16[256,1536]{1,0:T(8,128)(2,1)S(1)}, u32[]{:S(2)}, u32[]{:S(2)}) collective-permute-start(bf16[256,1536]{1,0:T(8,128)(2,1)S(1)} %copy-done.75), channel_id=1, source_target_pairs={{0,4},{4,0},{1,5},{5,1},{2,6},{6,2},{3,7},{7,3},{8,12},{12,8},{9,1... | collective-permute-start | bytes 2359304 | tf_op jit(solution)/shard_map/ppermute | solution.py:79
  553.0 40.8 %collective-permute-start.86 = (bf16[256,3200]{1,0:T(8,128)(2,1)S(1)}, bf16[256,3200]{1,0:T(8,128)(2,1)S(1)}, u32[]{:S(2)}, u32[]{:S(2)}) collective-permute-start(bf16[256,3200]{1,0:T(8,128)(2,1)S(1)} %slice.681), channel_id=1, source_target_pairs={{0,1},{1,0},{2,3},{3,2},{4,5},{5,4},{6,7},{7,6},{8,9},{9,8},{10,11... | collective-permute-start | bytes 4915208 | tf_op jit(solution)/shard_map/ppermute | solution.py:79
  599.1 33.4 %collective-permute-start.95 = (bf16[128,3200]{1,0:T(8,128)(2,1)S(1)}, bf16[128,3200]{1,0:T(8,128)(2,1)S(1)}, u32[]{:S(2)}, u32[]{:S(2)}) collective-permute-start(bf16[128,3200]{1,0:T(8,128)(2,1)S(1)} %slice.697), channel_id=1, source_target_pairs={{0,4},{4,0},{1,5},{5,1},{2,6},{6,2},{3,7},{7,3},{8,12},{12,8},{9,1... | collective-permute-start | bytes 2457608 | tf_op jit(solution)/shard_map/ppermute | solution.py:79
  615.9 29.0 %collective-permute-start.84 = (bf16[128,3200]{1,0:T(8,128)(2,1)S(1)}, bf16[128,3200]{1,0:T(8,128)(2,1)S(1)}, u32[]{:S(2)}, u32[]{:S(2)}) collective-permute-start(bf16[128,3200]{1,0:T(8,128)(2,1)S(1)} %slice.675), channel_id=1, source_target_pairs={{0,2},{2,0},{1,3},{3,1},{4,6},{6,4},{5,7},{7,5},{8,10},{10,8},{9,1... | collective-permute-start | bytes 2457608 | tf_op jit(solution)/shard_map/ppermute | solution.py:79
  643.3 26.2 %collective-permute-start.96 = (bf16[64,3200]{1,0:T(8,128)(2,1)S(1)}, bf16[64,3200]{1,0:T(8,128)(2,1)S(1)}, u32[]{:S(2)}, u32[]{:S(2)}) collective-permute-start(bf16[64,3200]{1,0:T(8,128)(2,1)S(1)} %slice.699), channel_id=1, source_target_pairs={{0,2},{2,0},{1,3},{3,1},{4,6},{6,4},{5,7},{7,5},{8,10},{10,8},{9,1... | collective-permute-start | bytes 1228808 | tf_op jit(solution)/shard_map/ppermute | solution.py:79
  645.3 25.9 %collective-permute-start.85 = (bf16[64,3200]{1,0:T(8,128)(2,1)S(1)}, bf16[64,3200]{1,0:T(8,128)(2,1)}, u32[]{:S(2)}, u32[]{:S(2)}) collective-permute-start(bf16[64,3200]{1,0:T(8,128)(2,1)S(1)} %slice.677), channel_id=1, source_target_pairs={{0,4},{4,0},{1,5},{5,1},{2,6},{6,2},{3,7},{7,3},{8,12},{12,8},{9,1... | collective-permute-start | bytes 1228808 | tf_op jit(solution)/shard_map/ppermute | solution.py:79
  663.0 69.0 %collective-permute-start.75 = (bf16[2,128,2048]{2,1,0:T(8,128)(2,1)}, bf16[2,128,2048]{2,1,0:T(8,128)(2,1)}, u32[]{:S(2)}, u32[]{:S(2)}) collective-permute-start(bf16[2,128,2048]{2,1,0:T(8,128)(2,1)} %slice.497), channel_id=1, source_target_pairs={{0,2},{2,0},{1,3},{3,1},{4,6},{6,4},{5,7},{7,5},{8,10},{10,8},{9,1... | collective-permute-start | bytes 3145736 | tf_op jit(solution)/shard_map/ppermute | solution.py:79
  668.0 86.8 %collective-permute-start.81 = (bf16[2,128,2048]{2,1,0:T(8,128)(2,1)S(1)}, bf16[2,128,2048]{2,1,0:T(8,128)(2,1)S(1)}, u32[]{:S(2)}, u32[]{:S(2)}) collective-permute-start(bf16[2,128,2048]{2,1,0:T(8,128)(2,1)S(1)} %fusion.136), channel_id=1, source_target_pairs={{0,2},{2,0},{1,3},{3,1},{4,6},{6,4},{5,7},{7,5},{8,10},{10,8},{9,1... | collective-permute-start | bytes 3145736 | tf_op jit(solution)/shard_map/ppermute | solution.py:79
  670.5 60.0 %collective-permute-start.98 = (bf16[2,128,2048]{2,1,0:T(8,128)(2,1)S(1)}, bf16[2,128,2048]{2,1,0:T(8,128)(2,1)S(1)}, u32[]{:S(2)}, u32[]{:S(2)}) collective-permute-start(bf16[2,128,2048]{2,1,0:T(8,128)(2,1)S(1)} %slice.705), channel_id=1, source_target_pairs={{0,2},{2,0},{1,3},{3,1},{4,6},{6,4},{5,7},{7,5},{8,10},{10,8},{9,1... | collective-permute-start | bytes 3145736 | tf_op jit(solution)/shard_map/ppermute | solution.py:79
  671.2 59.8 %collective-permute-start.100 = (bf16[2,128,2048]{2,1,0:T(8,128)(2,1)S(1)}, bf16[2,128,2048]{2,1,0:T(8,128)(2,1)S(1)}, u32[]{:S(2)}, u32[]{:S(2)}) collective-permute-start(bf16[2,128,2048]{2,1,0:T(8,128)(2,1)S(1)} %slice.709), channel_id=1, source_target_pairs={{0,4},{4,0},{1,5},{5,1},{2,6},{6,2},{3,7},{7,3},{8,12},{12,8},{9,1... | collective-permute-start | bytes 3145736 | tf_op jit(solution)/shard_map/ppermute | solution.py:79
  771.6 30.5 %collective-permute-start.109 = (bf16[256,1536]{1,0:T(8,128)(2,1)S(1)}, bf16[256,1536]{1,0:T(8,128)(2,1)S(1)}, u32[]{:S(2)}, u32[]{:S(2)}) collective-permute-start(bf16[256,1536]{1,0:T(8,128)(2,1)S(1)} %copy-done.76), channel_id=1, source_target_pairs={{0,24},{8,0},{16,8},{24,16},{1,25},{9,1},{17,9},{25,17},{2,26},{10... | collective-permute-start | bytes 2359304 | tf_op jit(solution)/shard_map/ppermute | solution.py:79
  773.0 78.8 %collective-permute-start.110 = (bf16[256,1536]{1,0:T(8,128)(2,1)S(1)}, bf16[256,1536]{1,0:T(8,128)(2,1)S(1)}, u32[]{:S(2)}, u32[]{:S(2)}) collective-permute-start(bf16[256,1536]{1,0:T(8,128)(2,1)S(1)} %copy-done.77), channel_id=1, source_target_pairs={{0,16},{8,24},{16,0},{24,8},{1,17},{9,25},{17,1},{25,9},{2,18},{10... | collective-permute-start | bytes 2359304 | tf_op jit(solution)/shard_map/ppermute | solution.py:79
  775.6 76.2 %collective-permute-start.111 = (bf16[256,1536]{1,0:T(8,128)(2,1)S(1)}, bf16[256,1536]{1,0:T(8,128)(2,1)S(1)}, u32[]{:S(2)}, u32[]{:S(2)}) collective-permute-start(bf16[256,1536]{1,0:T(8,128)(2,1)S(1)} %copy-done.78), channel_id=1, source_target_pairs={{0,8},{8,16},{16,24},{24,0},{1,9},{9,17},{17,25},{25,1},{2,10},{10... | collective-permute-start | bytes 2359304 | tf_op jit(solution)/shard_map/ppermute | solution.py:79
  (187 other events, 1867.6 us)
where the time goes:
time: 884 us; the launch traced here: 874 us
  waiting for transfers between devices  447 us (51%)
  matrix products  141 us (16%)
  local copies, waits for them, and re-layouts  113 us (13%)
  starting transfers between devices  87.1 us (10%)
  other arithmetic  82.1 us (9%)
    ppermute x112, waiting for transfers between devices, shift(): lax.ppermute(value, axis, [(i, (i + step) % count) for i in range(count)])  447 us
    ppermute x112, starting transfers between devices, shift(): lax.ppermute(value, axis, [(i, (i + step) % count) for i in range(count)])  87.1 us
    unnamed x297, local copies, waits for them, and re-layouts  53.8 us
    dot_general x12, matrix products, tdot(): lax.dot_general(left, right, (((0,), (0,)), ((), ())), preferred_element_...  41.1 us
    dot_general x15, matrix products, dot_t(): lax.dot_general(left, right, (((1,), (1,)), ((), ())), preferred_element_...  37.1 us
    convert_element_type x37, other arithmetic, add_rounded(): return (left.astype(F32) + right.astype(F32)).astype(left.dtype)  27.5 us
  transfers between devices with their start and end apart: 112, of which 46 were waited for; matrix products, arithmetic and copies ran while one was open for 30% of the time, Pallas kernels for 0%

commit v1 on v0

--- a/solution.py
+++ b/solution.py
@@ -148,7 +148,10 @@
     for step in range(1, count + 1):
         k = step % count
         part = tdot(permuted[:, k * columns : (k + 1) * columns], upstream).astype(BF16)
-        local[k] = reduce_axes(part, reversed(hop_order(k)))
+        axes = hop_order(k)[::-1]
+        part = reduce_axes(part, axes[:1])
+        part = reduce_axes(part, axes[1:2])
+        local[k] = reduce_axes(part, axes[2:])
     local = [local[k] for k in range(count)]
     return reduce_ring(local, "z"), local
 
@@ -195,6 +198,17 @@
     factor = 1.0 / HEAD_WIDTH**0.5
     own_rows = w_query.shape[0]
 
+    lanes = 128
+    qkv_width = query_width + 2 * kv_width
+    gain_columns = jnp.pad(jnp.stack([attn_gain, ffn_gain], axis=1), ((0, 0), (0, lanes - 2)))
+    qkv_own = jnp.concatenate([w_query, w_key, w_value, gain_columns], axis=1)
+    qkv_ring = gather_ring(qkv_own, "z")
+    qkv_last = qkv_ring[-1]
+    tokens, positions, segment_ids = after(
+        (tokens, positions, segment_ids), qkv_ring[2 % size_z]
+    )
+    w_gate, w_up, w_down = after((w_gate, w_up, w_down), qkv_last)
+
     sizes = {"y": size_y, "x": size_x, "c": size_c}
     here = {"y": at_y, "x": at_x, "c": at_c}
     plane = jnp.arange(devices // size_z, dtype=jnp.int32)
@@ -207,7 +221,7 @@
             stride *= sizes[axis]
         row = back(at_z, slot, size_z) * size_y + at["y"]
         pieces.append((row * size_x + at["x"]) * size_c + at["c"])
-    piece = jnp.concatenate(pieces)
+    (piece,) = after((jnp.concatenate(pieces),), qkv_ring[1 % size_z])
     feature = (piece[:, None] * own_rows + jnp.arange(own_rows, dtype=jnp.int32)).reshape(-1)
     selector = (jnp.arange(width, dtype=jnp.int32)[:, None] == feature[None, :]).astype(BF16)
 
@@ -217,11 +231,6 @@
     def by_feature(value):
         return dot_t(value.astype(BF16), selector)
 
-    lanes = 128
-    qkv_width = query_width + 2 * kv_width
-    gain_columns = jnp.pad(jnp.stack([attn_gain, ffn_gain], axis=1), ((0, 0), (0, lanes - 2)))
-    qkv_own = jnp.concatenate([w_query, w_key, w_value, gain_columns], axis=1)
-    qkv_ring = gather_ring(qkv_own, "z")
     packed_slots = [gather_rows(part, k) for k, part in enumerate(qkv_ring)]
     slot_rows = width // size_z
     qkv_slots = [part[:, :qkv_width] for part in packed_slots]
@@ -388,9 +397,9 @@
                 )
             )
         pairs_y.append(rows_y)
-    ffn_own = [
-        reduce_ring([pairs_y[k][step] for k in range(size_y)], "y") for step in range(size_z)
-    ]
+    ffn_own = {}
+    for step in reversed(range(size_z)):
+        ffn_own[step] = reduce_ring([pairs_y[k][step] for k in range(size_y)], "y")
 
     gain_term_two = jnp.sum(d_h_two * normed_two, axis=0)
     cot_rows = cotangent.reshape(token_rows, width)
@@ -433,21 +442,14 @@
         ],
         axis=-1,
     )
+    steps_early = [k for k in range(size_z) if k >= 2]
+    blocks_early = after([ffn_own[k] for k in steps_early], kv_gradient)
+    ffn_sums = {k: shift(b, "z", -k) for k, b in zip(steps_early, blocks_early)}
+    for k in range(min(2, size_z)):
+        ffn_sums[k] = shift(ffn_own[k], "z", -k) if k else ffn_own[k]
     for axis in ("c", "x"):
         count = lax.axis_size(axis)
         kv_gradient = reduce_ring(jnp.split(kv_gradient, count, axis=1), axis)
-    out_cores, part_cores = after((out_cores, part_cores), kv_gradient)
-    out_late = reduce_axes(jnp.stack([out_cores[k] for k in late]), ("x",))
-    out_across = {k: out_early[n] for n, k in enumerate(early)}
-    out_across.update({k: out_late[n] for n, k in enumerate(late)})
-    ffn_out = out_across[1]
-    for k in range(2, size_z):
-        ffn_out = add_rounded(shift(ffn_out, "z"), out_across[k])
-    ffn_own = after(ffn_own, ffn_out)
-    ffn_out = shift(ffn_out, "z")
-    ffn_sums = [shift(b, "z", -step) if step else b for step, b in enumerate(ffn_own)]
-    part_even = reduce_axes(part_cores[0::2], ("x", "y"))
-    part_odd = reduce_axes(part_cores[1::2], ("y", "x"))
     dquery = (
         reverse_rotation(
             d_rquery.reshape(local_sequence, context_rows, QUERY_HEADS, HEAD_WIDTH),
@@ -497,24 +499,33 @@
     )
     grad_qkv, local = reduce_weight(left, right)
     grad_qkv = grad_qkv.astype(F32)
+    (out_cores,) = after((out_cores,), local[1 % size_z])
+    (part_cores,) = after((part_cores,), local[2 % size_z])
+    out_late = reduce_axes(jnp.stack([out_cores[k] for k in late]), ("x",))
+    out_across = {k: out_early[n] for n, k in enumerate(early)}
+    out_across.update({k: out_late[n] for n, k in enumerate(late)})
+    part_even = reduce_axes(part_cores[0::2], ("x", "y"))
+    part_odd = reduce_axes(part_cores[1::2], ("y", "x"))
     part_even, part_odd = after((part_even, part_odd), local[0])
     output_local = [(part_odd if k % 2 else part_even)[k // 2] for k in range(size_z)]
     grad_output = reduce_ring(output_local, "z").astype(F32)
-    (ffn_out,) = after((ffn_out,), local[0])
-    mixed = (resid + add_rounded(ffn_out, out_across[0]).astype(F32)).astype(BF16)
-    ffn_sums = after(ffn_sums, local[0])
+    out_local = after([out_across[k] for k in range(size_z)], local[0])
+    ffn_out = reduce_ring(out_local, "z")
+    mixed = (resid + ffn_out.astype(F32)).astype(BF16)
+    ffn_sums = after([ffn_sums[k] for k in range(size_z)], local[0])
     grad_gate = jnp.zeros((ff_rows, ff_width), F32)
     grad_up = jnp.zeros((ff_rows, ff_width), F32)
     grad_down_t = jnp.zeros((ff_rows, ff_width), F32)
     for step, block in enumerate(ffn_sums):
         start = ahead(at_z, step, size_z) * ff_own
-        block = block.astype(F32)
-        grad_gate = lax.dynamic_update_slice_in_dim(grad_gate, block[:, :ff_own], start, axis=1)
+        grad_gate = lax.dynamic_update_slice_in_dim(
+            grad_gate, block[:, :ff_own].astype(F32), start, axis=1
+        )
         grad_up = lax.dynamic_update_slice_in_dim(
-            grad_up, block[:, ff_own : 2 * ff_own], start, axis=1
+            grad_up, block[:, ff_own : 2 * ff_own].astype(F32), start, axis=1
         )
         grad_down_t = lax.dynamic_update_slice_in_dim(
-            grad_down_t, block[:, 2 * ff_own :], start, axis=1
+            grad_down_t, block[:, 2 * ff_own :].astype(F32), start, axis=1
         )
     grad_down = grad_down_t.T
     grad_tokens = d_resid + by_feature(norm_back(d_h_one, normed_one, inv_one, gain_one_rel))

time: 884 us -> 857 us (0.969)
  waiting for transfers between devices: 447 us -> 348 us
  local copies, waits for them, and re-layouts: 113 us -> 150 us
  other arithmetic: 82.1 us -> 106 us
    ppermute x112, waiting for transfers between devices: 447 us -> 348 us  [shift(): lax.ppermute(value, axis, [(i, (i + step) % count) for i in range(count)])]
    convert_element_type x0 -> x12, local copies, waits for them, and re-layouts: none -> 24.5 us  [the longest x4 8.2 us: layer(): block[:, :ff_own].astype(F32)]
    slice x16 -> x0, local copies, waits for them, and re-layouts: 13.1 us -> none  [the longest x8 5.59 us: layer(): block[:, 2 * ff_own:]]
    concatenate x17, other arithmetic: 11.1 us -> 22.8 us  [gather_rows(): piece = jnp.concatenate(gather_ring(piece, axis), axis=0)]
    dynamic_update_slice x12, local copies, waits for them, and re-layouts: 1.53 us -> 11.2 us  [the longest x4 4.43 us: layer(): lax.dynamic_update_slice_in_dim(grad_down_t, block[:, 2 * ff_own:].astype...]
    unnamed x297 -> x301, local copies, waits for them, and re-layouts: 53.8 us -> 54.9 us
  transfers between devices with their start and end apart: 112 -> 112, of which waited for: 46 -> 47; matrix products, arithmetic and copies ran while one was open for 30% -> 41% of each run, Pallas kernels for 0% -> 0%
where the time goes in v1:
time: 857 us; the launch traced here: 847 us
  waiting for transfers between devices  348 us (41%)
  local copies, waits for them, and re-layouts  150 us (18%)
  matrix products  144 us (17%)
  other arithmetic  106 us (12%)
  starting transfers between devices  94.7 us (11%)
    ppermute x112, waiting for transfers between devices, shift(): lax.ppermute(value, axis, [(i, (i + step) % count) for i in range(count)])  348 us
    ppermute x112, starting transfers between devices, shift(): lax.ppermute(value, axis, [(i, (i + step) % count) for i in range(count)])  94.7 us
    unnamed x301, local copies, waits for them, and re-layouts  54.9 us
    dot_general x15, matrix products, dot_t(): lax.dot_general(left, right, (((1,), (1,)), ((), ())), preferred_element_...  40 us
    dot_general x12, matrix products, tdot(): lax.dot_general(left, right, (((0,), (0,)), ((), ())), preferred_element_...  38.8 us
    convert_element_type x37, other arithmetic, add_rounded(): return (left.astype(F32) + right.astype(F32)).astype(left.dtype)  35 us
    concatenate x17, other arithmetic, gather_rows(): piece = jnp.concatenate(gather_ring(piece, axis), axis=0)  22.8 us
  transfers between devices with their start and end apart: 112, of which 47 were waited for; matrix products, arithmetic and copies ran while one was open for 41% of the time, Pallas kernels for 0%

profile of v1, /device:TPU:0, one launch (start us, length us, event | category | flops | bytes accessed | tf_op | source)
XLA Modules:
  0.0 846.8 jit_solution(12783716654217035196)
XLA Ops:
  8.6 8.0 collective-permute-done.2
  20.8 5.7 iota_compare_fusion
  29.4 17.0 %collective-permute-done.5 = bf16[64,3200]{1,0:T(8,128)(2,1)S(1)} collective-permute-done((bf16[64,3200]{1,0:T(8,128)(2,1)S(1)}, bf16[64,3200]{1,0:T(8,128)(2,1)S(1)}, u32[]{:S(2)}, u32[]{:S(2)}) %collective-permute-start.5) | collective-permute-done | bytes 409632 | tf_op jit(solution)/shard_map/ppermute | solution.py:79
  57.2 3.7 collective-permute-done.11
  63.5 10.8 %collective-permute-done.8 = bf16[64,3200]{1,0:T(8,128)(2,1)S(1)} collective-permute-done((bf16[64,3200]{1,0:T(8,128)(2,1)S(1)}, bf16[64,3200]{1,0:T(8,128)(2,1)S(1)}, u32[]{:S(2)}, u32[]{:S(2)}) %collective-permute-start.8) | collective-permute-done | bytes 409632 | tf_op jit(solution)/shard_map/ppermute | solution.py:79
  90.0 11.5 %collective-permute-done.12 = bf16[64,3200]{1,0:T(8,128)(2,1)S(1)} collective-permute-done((bf16[64,3200]{1,0:T(8,128)(2,1)S(1)}, bf16[64,3200]{1,0:T(8,128)(2,1)S(1)}, u32[]{:S(2)}, u32[]{:S(2)}) %collective-permute-start.12) | collective-permute-done | bytes 409632 | tf_op jit(solution)/shard_map/ppermute | solution.py:79
  106.9 7.6 collective-permute-done.21
  134.8 4.6 multiply_convert_fusion.14
  217.6 5.2 collective-permute-done.68
  229.0 14.4 %collective-permute-done.41 = bf16[256,1536]{0,1:T(8,128)(2,1)S(1)} collective-permute-done((bf16[256,1536]{0,1:T(8,128)(2,1)}, bf16[256,1536]{0,1:T(8,128)(2,1)S(1)}, u32[]{:S(2)}, u32[]{:S(2)}) %collective-permute-start.41) | collective-permute-done | bytes 786464 | tf_op jit(solution)/shard_map/ppermute | solution.py:79
  246.0 14.3 %collective-permute-done.42 = bf16[256,1536]{0,1:T(8,128)(2,1)S(1)} collective-permute-done((bf16[256,1536]{0,1:T(8,128)(2,1)}, bf16[256,1536]{0,1:T(8,128)(2,1)S(1)}, u32[]{:S(2)}, u32[]{:S(2)}) %collective-permute-start.42) | collective-permute-done | bytes 786464 | tf_op jit(solution)/shard_map/ppermute | solution.py:79
  262.2 14.0 %collective-permute-done.43 = bf16[256,1536]{0,1:T(8,128)(2,1)S(1)} collective-permute-done((bf16[256,1536]{0,1:T(8,128)(2,1)}, bf16[256,1536]{0,1:T(8,128)(2,1)S(1)}, u32[]{:S(2)}, u32[]{:S(2)}) %collective-permute-start.43) | collective-permute-done | bytes 786464 | tf_op jit(solution)/shard_map/ppermute | solution.py:79
  277.1 13.8 %collective-permute-done.50 = bf16[128,2048]{1,0:T(8,128)(2,1)S(1)} collective-permute-done((bf16[128,2048]{1,0:T(8,128)(2,1)S(1)}, bf16[128,2048]{1,0:T(8,128)(2,1)S(1)}, u32[]{:S(2)}, u32[]{:S(2)}) %collective-permute-start.50) | collective-permute-done | bytes 524320 | tf_op jit(solution)/shard_map/ppermute | solution.py:79
  301.9 3.9 collective-permute-done.51
  311.7 5.3 collective-permute-done.70
  322.0 6.3 collective-permute-done.60
  331.2 7.8 collective-permute-done.45
  339.2 3.9 collective-permute-done.53
  362.0 3.7 fusion.71
  397.2 9.5 %convolution_convert_fusion.12 = bf16[2048,512]{1,0:T(8,128)(2,1)} fusion(bf16[2048,2048]{1,0:T(8,128)(2,1)} %constant_dynamic-update-slice_fusion.28, bf16[2048,512]{0,1:T(8,128)(2,1)S(1)} %get-tuple-element.131), kind=kOutput, calls=%fused_computation.57 | convolution fusion | flops 4296015872 | bytes 12582912 | tf_op jit(solution)/shard_map/dot_general | solution.py:58
  408.0 9.5 %convolution_convert_fusion.11 = bf16[2048,512]{1,0:T(8,128)(2,1)} fusion(bf16[2048,2048]{1,0:T(8,128)(2,1)} %constant_dynamic-update-slice_fusion.28, bf16[2048,512]{0,1:T(8,128)(2,1)S(1)} %get-tuple-element.143), kind=kOutput, calls=%fused_computation.56 | convolution fusion | flops 4296015872 | bytes 12582912 | tf_op jit(solution)/shard_map/dot_general | solution.py:58
  417.5 5.6 collective-permute-done.49
  424.5 9.5 %convolution_convert_fusion.10 = bf16[2048,512]{1,0:T(8,128)(2,1)} fusion(bf16[2048,2048]{1,0:T(8,128)(2,1)} %constant_dynamic-update-slice_fusion.40, bf16[2048,512]{0,1:T(8,128)(2,1)S(1)} %get-tuple-element.175), kind=kOutput, calls=%fused_computation.55 | convolution fusion | flops 4296015872 | bytes 12582912 | tf_op jit(solution)/shard_map/dot_general | solution.py:58
  434.0 4.8 collective-permute-done.58
  440.2 6.8 convolution_convert_fusion
  447.0 6.7 collective-permute-done.67
  461.7 4.4 fusion.54
  468.2 5.1 fusion.5
  473.3 5.4 fusion.120
  478.7 5.6 fusion.14
  511.3 5.9 collective-permute-done.76
  543.9 12.4 %collective-permute-done.108 = bf16[256,1536]{1,0:T(8,128)(2,1)} collective-permute-done((bf16[256,1536]{1,0:T(8,128)(2,1)}, bf16[256,1536]{1,0:T(8,128)(2,1)}, u32[]{:S(2)}, u32[]{:S(2)}) %collective-permute-start.108) | collective-permute-done | bytes 786464 | tf_op jit(solution)/shard_map/ppermute | solution.py:79
  561.0 10.8 %collective-permute-done.109 = bf16[256,1536]{1,0:T(8,128)(2,1)S(1)} collective-permute-done((bf16[256,1536]{1,0:T(8,128)(2,1)S(1)}, bf16[256,1536]{1,0:T(8,128)(2,1)S(1)}, u32[]{:S(2)}, u32[]{:S(2)}) %collective-permute-start.109) | collective-permute-done | bytes 786464 | tf_op jit(solution)/shard_map/ppermute | solution.py:79
  574.5 5.0 fusion.49
  584.8 16.7 %collective-permute-done.78 = bf16[128,3200]{1,0:T(8,128)(2,1)S(1)} collective-permute-done((bf16[128,3200]{1,0:T(8,128)(2,1)S(1)}, bf16[128,3200]{1,0:T(8,128)(2,1)S(1)}, u32[]{:S(2)}, u32[]{:S(2)}) %collective-permute-start.78) | collective-permute-done | bytes 819232 | tf_op jit(solution)/shard_map/ppermute | solution.py:79
  604.4 16.3 %collective-permute-done.94 = bf16[128,3200]{1,0:T(8,128)(2,1)S(1)} collective-permute-done((bf16[128,3200]{1,0:T(8,128)(2,1)S(1)}, bf16[128,3200]{1,0:T(8,128)(2,1)S(1)}, u32[]{:S(2)}, u32[]{:S(2)}) %collective-permute-start.94) | collective-permute-done | bytes 819232 | tf_op jit(solution)/shard_map/ppermute | solution.py:79
  621.5 9.9 %collective-permute-done.79 = bf16[64,3200]{1,0:T(8,128)(2,1)S(1)} collective-permute-done((bf16[64,3200]{1,0:T(8,128)(2,1)S(1)}, bf16[64,3200]{1,0:T(8,128)(2,1)S(1)}, u32[]{:S(2)}, u32[]{:S(2)}) %collective-permute-start.79) | collective-permute-done | bytes 409632 | tf_op jit(solution)/shard_map/ppermute | solution.py:79
  635.1 7.0 collective-permute-done.91
  642.1 6.1 collective-permute-done.88
  649.0 5.7 add_convert_fusion.1
  654.8 5.5 add_convert_fusion
  660.9 27.3 %collective-permute-done.92 = bf16[64,3200]{1,0:T(8,128)(2,1)} collective-permute-done((bf16[64,3200]{1,0:T(8,128)(2,1)S(1)}, bf16[64,3200]{1,0:T(8,128)(2,1)}, u32[]{:S(2)}, u32[]{:S(2)}) %collective-permute-start.92) | collective-permute-done | bytes 409632 | tf_op jit(solution)/shard_map/ppermute | solution.py:79
  689.4 12.7 %collective-permute-start.96 = (bf16[64,3200]{1,0:T(8,128)(2,1)S(1)}, bf16[64,3200]{1,0:T(8,128)(2,1)S(1)}, u32[]{:S(2)}, u32[]{:S(2)}) collective-permute-start(bf16[64,3200]{1,0:T(8,128)(2,1)S(1)} %add_convert_fusion.37), channel_id=1, source_target_pairs={{0,8},{8,16},{16,24},{24,0},{1,9},{9,17},{17,25},{25,1},{2,10},{10... | collective-permute-start | bytes 1228808 | tf_op jit(solution)/shard_map/ppermute | solution.py:79
  761.0 14.1 %collective-permute-done.98 = bf16[2,128,2048]{2,1,0:T(8,128)(2,1)} collective-permute-done((bf16[2,128,2048]{2,1,0:T(8,128)(2,1)}, bf16[2,128,2048]{2,1,0:T(8,128)(2,1)}, u32[]{:S(2)}, u32[]{:S(2)}) %collective-permute-start.98) | collective-permute-done | bytes 1048608 | tf_op jit(solution)/shard_map/ppermute | solution.py:79
  785.0 4.1 collective-permute-done.99
  800.2 4.1 collective-permute-done.102
  805.2 10.1 %collective-permute-done.85 = bf16[128,2048]{1,0:T(8,128)(2,1)} collective-permute-done((bf16[128,2048]{1,0:T(8,128)(2,1)}, bf16[128,2048]{1,0:T(8,128)(2,1)}, u32[]{:S(2)}, u32[]{:S(2)}) %collective-permute-start.85) | collective-permute-done | bytes 524320 | tf_op jit(solution)/shard_map/ppermute | solution.py:79
  822.1 11.2 %collective-permute-done.86 = bf16[128,2048]{1,0:T(8,128)(2,1)S(1)} collective-permute-done((bf16[128,2048]{1,0:T(8,128)(2,1)S(1)}, bf16[128,2048]{1,0:T(8,128)(2,1)S(1)}, u32[]{:S(2)}, u32[]{:S(2)}) %collective-permute-start.86) | collective-permute-done | bytes 524320 | tf_op jit(solution)/shard_map/ppermute | solution.py:79
  (767 shorter events, 424.0 us)
Async XLA Ops:
  18.5 42.4 %collective-permute-start.3 = (bf16[128,3200]{1,0:T(8,128)(2,1)}, bf16[128,3200]{1,0:T(8,128)(2,1)}, u32[]{:S(2)}, u32[]{:S(2)}) collective-permute-start(bf16[128,3200]{1,0:T(8,128)(2,1)} %pad_maximum_fusion.22), channel_id=1, source_target_pairs={{0,2},{2,0},{1,3},{3,1},{4,6},{6,4},{5,7},{7,5},{8,10},{10,8},{9,1... | collective-permute-start | bytes 2457608 | tf_op jit(solution)/shard_map/ppermute | solution.py:79
  26.5 22.4 %collective-permute-start.1 = (bf16[64,3200]{1,0:T(8,128)(2,1)S(1)}, bf16[64,3200]{1,0:T(8,128)(2,1)S(1)}, u32[]{:S(2)}, u32[]{:S(2)}) collective-permute-start(bf16[64,3200]{1,0:T(8,128)(2,1)S(1)} %collective-permute-done), channel_id=1, source_target_pairs={{0,8},{8,16},{16,24},{24,0},{1,9},{9,17},{17,25},{25,1},{2,10},{10... | collective-permute-start | bytes 1228808 | tf_op jit(solution)/shard_map/ppermute | solution.py:79
  47.4 41.3 %collective-permute-start.6 = (bf16[128,3200]{1,0:T(8,128)(2,1)}, bf16[128,3200]{1,0:T(8,128)(2,1)}, u32[]{:S(2)}, u32[]{:S(2)}) collective-permute-start(bf16[128,3200]{1,0:T(8,128)(2,1)} %pad_maximum_fusion.23), channel_id=1, source_target_pairs={{0,4},{4,0},{1,5},{5,1},{2,6},{6,2},{3,7},{7,3},{8,12},{12,8},{9,1... | collective-permute-start | bytes 2457608 | tf_op jit(solution)/shard_map/ppermute | solution.py:79
  52.9 21.5 %collective-permute-start.8 = (bf16[64,3200]{1,0:T(8,128)(2,1)S(1)}, bf16[64,3200]{1,0:T(8,128)(2,1)S(1)}, u32[]{:S(2)}, u32[]{:S(2)}) collective-permute-start(bf16[64,3200]{1,0:T(8,128)(2,1)S(1)} %collective-permute-done.1), channel_id=1, source_target_pairs={{0,4},{4,0},{1,5},{5,1},{2,6},{6,2},{3,7},{7,3},{8,12},{12,8},{9,1... | collective-permute-start | bytes 1228808 | tf_op jit(solution)/shard_map/ppermute | solution.py:79
  60.9 26.2 %collective-permute-start.19 = (bf16[64,2048]{1,0:T(8,128)(2,1)S(1)}, bf16[64,2048]{1,0:T(8,128)(2,1)}, u32[]{:S(2)}, u32[]{:S(2)}) collective-permute-start(bf16[64,2048]{1,0:T(8,128)(2,1)S(1)} %copy-done.44), channel_id=1, source_target_pairs={{0,8},{8,16},{16,24},{24,0},{1,9},{9,17},{17,25},{25,1},{2,10},{10... | collective-permute-start | bytes 786440 | tf_op jit(solution)/shard_map/ppermute | solution.py:79
  63.5 59.0 %collective-permute-start.4 = (bf16[256,3200]{1,0:T(8,128)(2,1)}, bf16[256,3200]{1,0:T(8,128)(2,1)}, u32[]{:S(2)}, u32[]{:S(2)}) collective-permute-start(bf16[256,3200]{1,0:T(8,128)(2,1)} %pad_maximum_fusion.1), channel_id=1, source_target_pairs={{0,1},{1,0},{2,3},{3,2},{4,5},{5,4},{6,7},{7,6},{8,9},{9,8},{10,11... | collective-permute-start | bytes 4915208 | tf_op jit(solution)/shard_map/ppermute | solution.py:79
  75.4 40.0 %collective-permute-start.9 = (bf16[128,3200]{1,0:T(8,128)(2,1)}, bf16[128,3200]{1,0:T(8,128)(2,1)}, u32[]{:S(2)}, u32[]{:S(2)}) collective-permute-start(bf16[128,3200]{1,0:T(8,128)(2,1)} %pad_maximum_fusion.24), channel_id=1, source_target_pairs={{0,2},{2,0},{1,3},{3,1},{4,6},{6,4},{5,7},{7,5},{8,10},{10,8},{9,1... | collective-permute-start | bytes 2457608 | tf_op jit(solution)/shard_map/ppermute | solution.py:79
  89.9 36.5 %collective-permute-start.7 = (bf16[256,3200]{1,0:T(8,128)(2,1)S(1)}, bf16[256,3200]{1,0:T(8,128)(2,1)S(1)}, u32[]{:S(2)}, u32[]{:S(2)}) collective-permute-start(bf16[256,3200]{1,0:T(8,128)(2,1)S(1)} %pad_maximum_fusion.2), channel_id=1, source_target_pairs={{0,1},{1,0},{2,3},{3,2},{4,5},{5,4},{6,7},{7,6},{8,9},{9,8},{10,11... | collective-permute-start | bytes 4915208 | tf_op jit(solution)/shard_map/ppermute | solution.py:79
  114.5 76.7 %collective-permute-start.37 = (bf16[256,1536]{0,1:T(8,128)(2,1)}, bf16[256,1536]{0,1:T(8,128)(2,1)}, u32[]{:S(2)}, u32[]{:S(2)}) collective-permute-start(bf16[256,1536]{0,1:T(8,128)(2,1)} %pad_maximum_fusion.27), channel_id=1, source_target_pairs={{0,8},{8,16},{16,24},{24,0},{1,9},{9,17},{17,25},{25,1},{2,10},{10... | collective-permute-start | bytes 2359304 | tf_op jit(solution)/shard_map/ppermute | solution.py:79
  115.4 76.3 %collective-permute-start.38 = (bf16[256,1536]{0,1:T(8,128)(2,1)}, bf16[256,1536]{0,1:T(8,128)(2,1)}, u32[]{:S(2)}, u32[]{:S(2)}) collective-permute-start(bf16[256,1536]{0,1:T(8,128)(2,1)} %pad_maximum_fusion.28), channel_id=1, source_target_pairs={{0,16},{8,24},{16,0},{24,8},{1,17},{9,25},{17,1},{25,9},{2,18},{10... | collective-permute-start | bytes 2359304 | tf_op jit(solution)/shard_map/ppermute | solution.py:79
  119.9 73.8 %collective-permute-start.39 = (bf16[256,1536]{0,1:T(8,128)(2,1)}, bf16[256,1536]{0,1:T(8,128)(2,1)}, u32[]{:S(2)}, u32[]{:S(2)}) collective-permute-start(bf16[256,1536]{0,1:T(8,128)(2,1)} %pad_maximum_fusion.29), channel_id=1, source_target_pairs={{0,24},{8,0},{16,8},{24,16},{1,25},{9,1},{17,9},{25,17},{2,26},{10... | collective-permute-start | bytes 2359304 | tf_op jit(solution)/shard_map/ppermute | solution.py:79
  149.6 24.3 %collective-permute-start.28 = (bf16[64,2048]{1,0:T(8,128)(2,1)}, bf16[64,2048]{1,0:T(8,128)(2,1)S(1)}, u32[]{:S(2)}, u32[]{:S(2)}) collective-permute-start(bf16[64,2048]{1,0:T(8,128)(2,1)} %collective-permute-done.20), channel_id=1, source_target_pairs={{0,4},{4,0},{1,5},{5,1},{2,6},{6,2},{3,7},{7,3},{8,12},{12,8},{9,1... | collective-permute-start | bytes 786440 | tf_op jit(solution)/shard_map/ppermute | solution.py:79
  193.7 32.5 %collective-permute-start.40 = (bf16[256,1536]{0,1:T(8,128)(2,1)S(1)}, bf16[256,1536]{0,1:T(8,128)(2,1)S(1)}, u32[]{:S(2)}, u32[]{:S(2)}) collective-permute-start(bf16[256,1536]{0,1:T(8,128)(2,1)S(1)} %copy-done.34), channel_id=1, source_target_pairs={{0,4},{4,0},{1,5},{5,1},{2,6},{6,2},{3,7},{7,3},{8,12},{12,8},{9,1... | collective-permute-start | bytes 2359304 | tf_op jit(solution)/shard_map/ppermute | solution.py:79
  206.6 39.3 %collective-permute-start.34 = (bf16[128,2048]{1,0:T(8,128)(2,1)S(1)}, bf16[128,2048]{1,0:T(8,128)(2,1)S(1)}, u32[]{:S(2)}, u32[]{:S(2)}) collective-permute-start(bf16[128,2048]{1,0:T(8,128)(2,1)S(1)} %bitcast.210), channel_id=1, source_target_pairs={{0,8},{8,16},{16,24},{24,0},{1,9},{9,17},{17,25},{25,1},{2,10},{10... | collective-permute-start | bytes 1572872 | tf_op jit(solution)/shard_map/ppermute | solution.py:79
  209.3 67.1 %collective-permute-start.33 = (bf16[256,2048]{1,0:T(8,128)(2,1)S(1)}, bf16[256,2048]{1,0:T(8,128)(2,1)S(1)}, u32[]{:S(2)}, u32[]{:S(2)}) collective-permute-start(bf16[256,2048]{1,0:T(8,128)(2,1)S(1)} %pad_maximum_fusion.12), channel_id=1, source_target_pairs={{0,1},{1,0},{2,3},{3,2},{4,5},{5,4},{6,7},{7,6},{8,9},{9,8},{10,11... | collective-permute-start | bytes 3145736 | tf_op jit(solution)/shard_map/ppermute | solution.py:79
  212.4 78.6 %collective-permute-start.30 = (bf16[256,2048]{1,0:T(8,128)(2,1)S(1)}, bf16[256,2048]{1,0:T(8,128)(2,1)S(1)}, u32[]{:S(2)}, u32[]{:S(2)}) collective-permute-start(bf16[256,2048]{1,0:T(8,128)(2,1)S(1)} %pad_maximum_fusion.11), channel_id=1, source_target_pairs={{0,1},{1,0},{2,3},{3,2},{4,5},{5,4},{6,7},{7,6},{8,9},{9,8},{10,11... | collective-permute-start | bytes 3145736 | tf_op jit(solution)/shard_map/ppermute | solution.py:79
  226.2 34.1 %collective-permute-start.42 = (bf16[256,1536]{0,1:T(8,128)(2,1)}, bf16[256,1536]{0,1:T(8,128)(2,1)S(1)}, u32[]{:S(2)}, u32[]{:S(2)}) collective-permute-start(bf16[256,1536]{0,1:T(8,128)(2,1)} %collective-permute-done.38), channel_id=1, source_target_pairs={{0,4},{4,0},{1,5},{5,1},{2,6},{6,2},{3,7},{7,3},{8,12},{12,8},{9,1... | collective-permute-start | bytes 2359304 | tf_op jit(solution)/shard_map/ppermute | solution.py:79
  243.4 32.8 %collective-permute-start.43 = (bf16[256,1536]{0,1:T(8,128)(2,1)}, bf16[256,1536]{0,1:T(8,128)(2,1)S(1)}, u32[]{:S(2)}, u32[]{:S(2)}) collective-permute-start(bf16[256,1536]{0,1:T(8,128)(2,1)} %collective-permute-done.39), channel_id=1, source_target_pairs={{0,4},{4,0},{1,5},{5,1},{2,6},{6,2},{3,7},{7,3},{8,12},{12,8},{9,1... | collective-permute-start | bytes 2359304 | tf_op jit(solution)/shard_map/ppermute | solution.py:79
  245.9 45.7 %collective-permute-start.27 = (bf16[256,2048]{1,0:T(8,128)(2,1)S(1)}, bf16[256,2048]{1,0:T(8,128)(2,1)S(1)}, u32[]{:S(2)}, u32[]{:S(2)}) collective-permute-start(bf16[256,2048]{1,0:T(8,128)(2,1)S(1)} %pad_maximum_fusion.10), channel_id=1, source_target_pairs={{0,1},{1,0},{2,3},{3,2},{4,5},{5,4},{6,7},{7,6},{8,9},{9,8},{10,11... | collective-permute-start | bytes 3145736 | tf_op jit(solution)/shard_map/ppermute | solution.py:79
  276.5 29.4 %collective-permute-start.69 = (bf16[256,2048]{1,0:T(8,128)(2,1)S(1)}, bf16[256,2048]{1,0:T(8,128)(2,1)S(1)}, u32[]{:S(2)}, u32[]{:S(2)}) collective-permute-start(bf16[256,2048]{1,0:T(8,128)(2,1)S(1)} %pad_maximum_fusion.19), channel_id=1, source_target_pairs={{0,1},{1,0},{2,3},{3,2},{4,5},{5,4},{6,7},{7,6},{8,9},{9,8},{10,11... | collective-permute-start | bytes 3145736 | tf_op jit(solution)/shard_map/ppermute | solution.py:79
  291.0 37.4 %collective-permute-start.36 = (bf16[256,2048]{1,0:T(8,128)(2,1)S(1)}, bf16[256,2048]{1,0:T(8,128)(2,1)S(1)}, u32[]{:S(2)}, u32[]{:S(2)}) collective-permute-start(bf16[256,2048]{1,0:T(8,128)(2,1)S(1)} %pad_maximum_fusion.13), channel_id=1, source_target_pairs={{0,1},{1,0},{2,3},{3,2},{4,5},{5,4},{6,7},{7,6},{8,9},{9,8},{10,11... | collective-permute-start | bytes 3145736 | tf_op jit(solution)/shard_map/ppermute | solution.py:79
  305.9 37.7 %collective-permute-start.52 = (bf16[256,2048]{1,0:T(8,128)(2,1)S(1)}, bf16[256,2048]{1,0:T(8,128)(2,1)S(1)}, u32[]{:S(2)}, u32[]{:S(2)}) collective-permute-start(bf16[256,2048]{1,0:T(8,128)(2,1)S(1)} %pad_maximum_fusion.15), channel_id=1, source_target_pairs={{0,1},{1,0},{2,3},{3,2},{4,5},{5,4},{6,7},{7,6},{8,9},{9,8},{10,11... | collective-permute-start | bytes 3145736 | tf_op jit(solution)/shard_map/ppermute | solution.py:79
  307.5 20.7 %collective-permute-start.60 = (bf16[128,2048]{1,0:T(8,128)(2,1)S(1)}, bf16[128,2048]{1,0:T(8,128)(2,1)S(1)}, u32[]{:S(2)}, u32[]{:S(2)}) collective-permute-start(bf16[128,2048]{1,0:T(8,128)(2,1)S(1)} %collective-permute-done.59), channel_id=1, source_target_pairs={{0,2},{2,0},{1,3},{3,1},{4,6},{6,4},{5,7},{7,5},{8,10},{10,8},{9,1... | collective-permute-start | bytes 1572872 | tf_op jit(solution)/shard_map/ppermute | solution.py:79
  317.1 29.5 %collective-permute-start.71 = (bf16[256,2048]{1,0:T(8,128)(2,1)S(1)}, bf16[256,2048]{1,0:T(8,128)(2,1)S(1)}, u32[]{:S(2)}, u32[]{:S(2)}) collective-permute-start(bf16[256,2048]{1,0:T(8,128)(2,1)S(1)} %pad_maximum_fusion.20), channel_id=1, source_target_pairs={{0,1},{1,0},{2,3},{3,2},{4,5},{5,4},{6,7},{7,6},{8,9},{9,8},{10,11... | collective-permute-start | bytes 3145736 | tf_op jit(solution)/shard_map/ppermute | solution.py:79
  328.3 32.6 %collective-permute-start.61 = (bf16[256,2048]{1,0:T(8,128)(2,1)S(1)}, bf16[256,2048]{1,0:T(8,128)(2,1)S(1)}, u32[]{:S(2)}, u32[]{:S(2)}) collective-permute-start(bf16[256,2048]{1,0:T(8,128)(2,1)S(1)} %pad_maximum_fusion.17), channel_id=1, source_target_pairs={{0,1},{1,0},{2,3},{3,2},{4,5},{5,4},{6,7},{7,6},{8,9},{9,8},{10,11... | collective-permute-start | bytes 3145736 | tf_op jit(solution)/shard_map/ppermute | solution.py:79
  339.1 22.9 %collective-permute-start.46 = (bf16[256,2048]{1,0:T(8,128)(2,1)S(1)}, bf16[256,2048]{1,0:T(8,128)(2,1)S(1)}, u32[]{:S(2)}, u32[]{:S(2)}) collective-permute-start(bf16[256,2048]{1,0:T(8,128)(2,1)S(1)} %pad_maximum_fusion.14), channel_id=1, source_target_pairs={{0,1},{1,0},{2,3},{3,2},{4,5},{5,4},{6,7},{7,6},{8,9},{9,8},{10,11... | collective-permute-start | bytes 3145736 | tf_op jit(solution)/shard_map/ppermute | solution.py:79
  355.0 21.2 %collective-permute-start.72 = (bf16[256,2048]{1,0:T(8,128)(2,1)}, bf16[256,2048]{1,0:T(8,128)(2,1)S(1)}, u32[]{:S(2)}, u32[]{:S(2)}) collective-permute-start(bf16[256,2048]{1,0:T(8,128)(2,1)} %slice.653), channel_id=1, source_target_pairs={{0,1},{1,0},{2,3},{3,2},{4,5},{5,4},{6,7},{7,6},{8,9},{9,8},{10,11... | collective-permute-start | bytes 3145736 | tf_op jit(solution)/shard_map/ppermute | solution.py:79
  376.6 70.4 %collective-permute-start.73 = (bf16[128,2048]{1,0:T(8,128)(2,1)S(1)}, bf16[128,2048]{1,0:T(8,128)(2,1)S(1)}, u32[]{:S(2)}, u32[]{:S(2)}) collective-permute-start(bf16[128,2048]{1,0:T(8,128)(2,1)S(1)} %slice.655), channel_id=1, source_target_pairs={{0,2},{2,0},{1,3},{3,1},{4,6},{6,4},{5,7},{7,5},{8,10},{10,8},{9,1... | collective-permute-start | bytes 1572872 | tf_op jit(solution)/shard_map/ppermute | solution.py:79
  383.8 23.1 %collective-permute-start.56 = (bf16[256,2048]{1,0:T(8,128)(2,1)S(1)}, bf16[256,2048]{1,0:T(8,128)(2,1)S(1)}, u32[]{:S(2)}, u32[]{:S(2)}) collective-permute-start(bf16[256,2048]{1,0:T(8,128)(2,1)S(1)} %slice.641), channel_id=1, source_target_pairs={{0,1},{1,0},{2,3},{3,2},{4,5},{5,4},{6,7},{7,6},{8,9},{9,8},{10,11... | collective-permute-start | bytes 3145736 | tf_op jit(solution)/shard_map/ppermute | solution.py:79
  395.8 27.6 %collective-permute-start.65 = (bf16[256,2048]{1,0:T(8,128)(2,1)S(1)}, bf16[256,2048]{1,0:T(8,128)(2,1)S(1)}, u32[]{:S(2)}, u32[]{:S(2)}) collective-permute-start(bf16[256,2048]{1,0:T(8,128)(2,1)S(1)} %slice.647), channel_id=1, source_target_pairs={{0,1},{1,0},{2,3},{3,2},{4,5},{5,4},{6,7},{7,6},{8,9},{9,8},{10,11... | collective-permute-start | bytes 3145736 | tf_op jit(solution)/shard_map/ppermute | solution.py:79
  492.5 155.9 %collective-permute-start.74 = (bf16[4,256,2048]{2,1,0:T(8,128)(2,1)}, bf16[4,256,2048]{2,1,0:T(8,128)(2,1)}, u32[]{:S(2)}, u32[]{:S(2)}) collective-permute-start(bf16[4,256,2048]{2,1,0:T(8,128)(2,1)} %slice.657), channel_id=1, source_target_pairs={{0,1},{1,0},{2,3},{3,2},{4,5},{5,4},{6,7},{7,6},{8,9},{9,8},{10,11... | collective-permute-start | bytes 12582920 | tf_op jit(solution)/shard_map/ppermute | solution.py:79
  496.2 158.5 %collective-permute-start.97 = (bf16[4,256,2048]{2,1,0:T(8,128)(2,1)}, bf16[4,256,2048]{2,1,0:T(8,128)(2,1)}, u32[]{:S(2)}, u32[]{:S(2)}) collective-permute-start(bf16[4,256,2048]{2,1,0:T(8,128)(2,1)} %slice.703), channel_id=1, source_target_pairs={{0,1},{1,0},{2,3},{3,2},{4,5},{5,4},{6,7},{7,6},{8,9},{9,8},{10,11... | collective-permute-start | bytes 12582920 | tf_op jit(solution)/shard_map/ppermute | solution.py:79
  501.9 36.3 %collective-permute-start.105 = (bf16[256,1536]{1,0:T(8,128)(2,1)}, bf16[256,1536]{1,0:T(8,128)(2,1)}, u32[]{:S(2)}, u32[]{:S(2)}) collective-permute-start(bf16[256,1536]{1,0:T(8,128)(2,1)} %pad_maximum_fusion.31), channel_id=1, source_target_pairs={{0,4},{4,0},{1,5},{5,1},{2,6},{6,2},{3,7},{7,3},{8,12},{12,8},{9,1... | collective-permute-start | bytes 2359304 | tf_op jit(solution)/shard_map/ppermute | solution.py:79
  504.7 37.0 %collective-permute-start.106 = (bf16[256,1536]{1,0:T(8,128)(2,1)}, bf16[256,1536]{1,0:T(8,128)(2,1)}, u32[]{:S(2)}, u32[]{:S(2)}) collective-permute-start(bf16[256,1536]{1,0:T(8,128)(2,1)} %pad_maximum_fusion.32), channel_id=1, source_target_pairs={{0,4},{4,0},{1,5},{5,1},{2,6},{6,2},{3,7},{7,3},{8,12},{12,8},{9,1... | collective-permute-start | bytes 2359304 | tf_op jit(solution)/shard_map/ppermute | solution.py:79
  517.1 39.2 %collective-permute-start.108 = (bf16[256,1536]{1,0:T(8,128)(2,1)}, bf16[256,1536]{1,0:T(8,128)(2,1)}, u32[]{:S(2)}, u32[]{:S(2)}) collective-permute-start(bf16[256,1536]{1,0:T(8,128)(2,1)} %pad_maximum_fusion.33), channel_id=1, source_target_pairs={{0,4},{4,0},{1,5},{5,1},{2,6},{6,2},{3,7},{7,3},{8,12},{12,8},{9,1... | collective-permute-start | bytes 2359304 | tf_op jit(solution)/shard_map/ppermute | solution.py:79
  539.1 32.8 %collective-permute-start.109 = (bf16[256,1536]{1,0:T(8,128)(2,1)S(1)}, bf16[256,1536]{1,0:T(8,128)(2,1)S(1)}, u32[]{:S(2)}, u32[]{:S(2)}) collective-permute-start(bf16[256,1536]{1,0:T(8,128)(2,1)S(1)} %copy-done.86), channel_id=1, source_target_pairs={{0,4},{4,0},{1,5},{5,1},{2,6},{6,2},{3,7},{7,3},{8,12},{12,8},{9,1... | collective-permute-start | bytes 2359304 | tf_op jit(solution)/shard_map/ppermute | solution.py:79
  541.7 37.8 %collective-permute-start.77 = (bf16[256,3200]{1,0:T(8,128)(2,1)S(1)}, bf16[256,3200]{1,0:T(8,128)(2,1)S(1)}, u32[]{:S(2)}, u32[]{:S(2)}) collective-permute-start(bf16[256,3200]{1,0:T(8,128)(2,1)S(1)} %slice.666), channel_id=1, source_target_pairs={{0,1},{1,0},{2,3},{3,2},{4,5},{5,4},{6,7},{7,6},{8,9},{9,8},{10,11... | collective-permute-start | bytes 4915208 | tf_op jit(solution)/shard_map/ppermute | solution.py:79
  556.3 24.2 %collective-permute-start.89 = (bf16[256,3200]{1,0:T(8,128)(2,1)S(1)}, bf16[256,3200]{1,0:T(8,128)(2,1)S(1)}, u32[]{:S(2)}, u32[]{:S(2)}) collective-permute-start(bf16[256,3200]{1,0:T(8,128)(2,1)S(1)} %slice.686), channel_id=1, source_target_pairs={{0,1},{1,0},{2,3},{3,2},{4,5},{5,4},{6,7},{7,6},{8,9},{9,8},{10,11... | collective-permute-start | bytes 4915208 | tf_op jit(solution)/shard_map/ppermute | solution.py:79
  580.5 130.4 %collective-permute-start.107 = (bf16[256,1536]{1,0:T(8,128)(2,1)}, bf16[256,1536]{1,0:T(8,128)(2,1)}, u32[]{:S(2)}, u32[]{:S(2)}) collective-permute-start(bf16[256,1536]{1,0:T(8,128)(2,1)} %add_convert_fusion.20), channel_id=1, source_target_pairs={{0,24},{8,0},{16,8},{24,16},{1,25},{9,1},{17,9},{25,17},{2,26},{10... | collective-permute-start | bytes 2359304 | tf_op jit(solution)/shard_map/ppermute | solution.py:79
  603.6 30.3 %collective-permute-start.83 = (bf16[128,3200]{1,0:T(8,128)(2,1)S(1)}, bf16[128,3200]{1,0:T(8,128)(2,1)S(1)}, u32[]{:S(2)}, u32[]{:S(2)}) collective-permute-start(bf16[128,3200]{1,0:T(8,128)(2,1)S(1)} %slice.681), channel_id=1, source_target_pairs={{0,2},{2,0},{1,3},{3,1},{4,6},{6,4},{5,7},{7,5},{8,10},{10,8},{9,1... | collective-permute-start | bytes 2457608 | tf_op jit(solution)/shard_map/ppermute | solution.py:79
  642.1 71.6 %collective-permute-start.110 = (bf16[256,1536]{1,0:T(8,128)(2,1)}, bf16[256,1536]{1,0:T(8,128)(2,1)}, u32[]{:S(2)}, u32[]{:S(2)}) collective-permute-start(bf16[256,1536]{1,0:T(8,128)(2,1)} %add_convert_fusion.19), channel_id=1, source_target_pairs={{0,16},{8,24},{16,0},{24,8},{1,17},{9,25},{17,1},{25,9},{2,18},{10... | collective-permute-start | bytes 2359304 | tf_op jit(solution)/shard_map/ppermute | solution.py:79
  648.2 66.4 %collective-permute-start.111 = (bf16[256,1536]{1,0:T(8,128)(2,1)}, bf16[256,1536]{1,0:T(8,128)(2,1)}, u32[]{:S(2)}, u32[]{:S(2)}) collective-permute-start(bf16[256,1536]{1,0:T(8,128)(2,1)} %add_convert_fusion.18), channel_id=1, source_target_pairs={{0,8},{8,16},{16,24},{24,0},{1,9},{9,17},{17,25},{25,1},{2,10},{10... | collective-permute-start | bytes 2359304 | tf_op jit(solution)/shard_map/ppermute | solution.py:79
  654.7 33.5 %collective-permute-start.92 = (bf16[64,3200]{1,0:T(8,128)(2,1)S(1)}, bf16[64,3200]{1,0:T(8,128)(2,1)}, u32[]{:S(2)}, u32[]{:S(2)}) collective-permute-start(bf16[64,3200]{1,0:T(8,128)(2,1)S(1)} %add_convert_fusion.39), channel_id=1, source_target_pairs={{0,8},{8,16},{16,24},{24,0},{1,9},{9,17},{17,25},{25,1},{2,10},{10... | collective-permute-start | bytes 1228808 | tf_op jit(solution)/shard_map/ppermute | solution.py:79
  660.9 45.9 %collective-permute-start.84 = (bf16[64,3200]{1,0:T(8,128)(2,1)S(1)}, bf16[64,3200]{1,0:T(8,128)(2,1)S(1)}, u32[]{:S(2)}, u32[]{:S(2)}) collective-permute-start(bf16[64,3200]{1,0:T(8,128)(2,1)S(1)} %slice.683), channel_id=1, source_target_pairs={{0,4},{4,0},{1,5},{5,1},{2,6},{6,2},{3,7},{7,3},{8,12},{12,8},{9,1... | collective-permute-start | bytes 1228808 | tf_op jit(solution)/shard_map/ppermute | solution.py:79
  706.7 76.5 %collective-permute-start.80 = (bf16[2,128,2048]{2,1,0:T(8,128)(2,1)}, bf16[2,128,2048]{2,1,0:T(8,128)(2,1)}, u32[]{:S(2)}, u32[]{:S(2)}) collective-permute-start(bf16[2,128,2048]{2,1,0:T(8,128)(2,1)} %fusion.135), channel_id=1, source_target_pairs={{0,2},{2,0},{1,3},{3,1},{4,6},{6,4},{5,7},{7,5},{8,10},{10,8},{9,1... | collective-permute-start | bytes 3145736 | tf_op jit(solution)/shard_map/ppermute | solution.py:79
  709.3 72.0 %collective-permute-start.81 = (bf16[2,128,2048]{2,1,0:T(8,128)(2,1)}, bf16[2,128,2048]{2,1,0:T(8,128)(2,1)}, u32[]{:S(2)}, u32[]{:S(2)}) collective-permute-start(bf16[2,128,2048]{2,1,0:T(8,128)(2,1)} %slice.515), channel_id=1, source_target_pairs={{0,2},{2,0},{1,3},{3,1},{4,6},{6,4},{5,7},{7,5},{8,10},{10,8},{9,1... | collective-permute-start | bytes 3145736 | tf_op jit(solution)/shard_map/ppermute | solution.py:79
  710.9 64.2 %collective-permute-start.98 = (bf16[2,128,2048]{2,1,0:T(8,128)(2,1)}, bf16[2,128,2048]{2,1,0:T(8,128)(2,1)}, u32[]{:S(2)}, u32[]{:S(2)}) collective-permute-start(bf16[2,128,2048]{2,1,0:T(8,128)(2,1)} %slice.705), channel_id=1, source_target_pairs={{0,2},{2,0},{1,3},{3,1},{4,6},{6,4},{5,7},{7,5},{8,10},{10,8},{9,1... | collective-permute-start | bytes 3145736 | tf_op jit(solution)/shard_map/ppermute | solution.py:79
  713.8 65.3 %collective-permute-start.100 = (bf16[2,128,2048]{2,1,0:T(8,128)(2,1)}, bf16[2,128,2048]{2,1,0:T(8,128)(2,1)}, u32[]{:S(2)}, u32[]{:S(2)}) collective-permute-start(bf16[2,128,2048]{2,1,0:T(8,128)(2,1)} %slice.709), channel_id=1, source_target_pairs={{0,4},{4,0},{1,5},{5,1},{2,6},{6,2},{3,7},{7,3},{8,12},{12,8},{9,1... | collective-permute-start | bytes 3145736 | tf_op jit(solution)/shard_map/ppermute | solution.py:79
  (193 other events, 2141.8 us)

commit v2 on v1

--- a/solution.py
+++ b/solution.py
@@ -1,6 +1,8 @@
 import jax
 import jax.numpy as jnp
 from jax import lax
+from jax.experimental import pallas as pl
+from jax.experimental.pallas import tpu as pltpu
 from jax.sharding import Mesh
 from jax.sharding import PartitionSpec as P
 
@@ -167,6 +169,42 @@
 
 def after(values, *waits):
     return lax.optimization_barrier((tuple(values), waits))[0]
+
+
+def place_blocks(at_z, blocks):
+    count = len(blocks)
+    rows, packed = blocks[0].shape
+    columns = packed // 3
+
+    def kernel(at_ref, *refs):
+        sources, (gate, up, down) = refs[:count], refs[count:]
+        wanted = lax.rem(pl.program_id(0) + (count - at_ref[0]), jnp.int32(count))
+        for k in range(count):
+
+            @pl.when(wanted == k)
+            def _():
+                gate[...] = sources[k][:, :columns].astype(F32)
+                up[...] = sources[k][:, columns : 2 * columns].astype(F32)
+                down[...] = sources[k][:, 2 * columns :].astype(F32).T
+
+    whole = pl.BlockSpec((rows, packed), lambda b, at: (0, 0))
+    flat = pl.BlockSpec((rows, columns), lambda b, at: (0, b))
+    tall = pl.BlockSpec((columns, rows), lambda b, at: (b, 0))
+    return pl.pallas_call(
+        kernel,
+        grid_spec=pltpu.PrefetchScalarGridSpec(
+            num_scalar_prefetch=1,
+            grid=(count,),
+            in_specs=[whole] * count,
+            out_specs=[flat, flat, tall],
+        ),
+        out_shape=[
+            jax.ShapeDtypeStruct((rows, columns * count), F32),
+            jax.ShapeDtypeStruct((rows, columns * count), F32),
+            jax.ShapeDtypeStruct((columns * count, rows), F32),
+        ],
+        name="place_blocks",
+    )(at_z.astype(jnp.int32).reshape(1), *blocks)
 
 
 def layer(
@@ -513,21 +551,7 @@
     ffn_out = reduce_ring(out_local, "z")
     mixed = (resid + ffn_out.astype(F32)).astype(BF16)
     ffn_sums = after([ffn_sums[k] for k in range(size_z)], local[0])
-    grad_gate = jnp.zeros((ff_rows, ff_width), F32)
-    grad_up = jnp.zeros((ff_rows, ff_width), F32)
-    grad_down_t = jnp.zeros((ff_rows, ff_width), F32)
-    for step, block in enumerate(ffn_sums):
-        start = ahead(at_z, step, size_z) * ff_own
-        grad_gate = lax.dynamic_update_slice_in_dim(
-            grad_gate, block[:, :ff_own].astype(F32), start, axis=1
-        )
-        grad_up = lax.dynamic_update_slice_in_dim(
-            grad_up, block[:, ff_own : 2 * ff_own].astype(F32), start, axis=1
-        )
-        grad_down_t = lax.dynamic_update_slice_in_dim(
-            grad_down_t, block[:, 2 * ff_own :].astype(F32), start, axis=1
-        )
-    grad_down = grad_down_t.T
+    grad_gate, grad_up, grad_down = place_blocks(at_z, ffn_sums)
     grad_tokens = d_resid + by_feature(norm_back(d_h_one, normed_one, inv_one, gain_one_rel))
     return (
         mixed.reshape(local_sequence, context_rows, width),

time: 857 us -> 826 us (0.964)
  local copies, waits for them, and re-layouts: 150 us -> 98.6 us
  waiting for transfers between devices: 348 us -> 385 us
  other arithmetic: 106 us -> 87.7 us
    ppermute x112, waiting for transfers between devices: 348 us -> 385 us  [shift(): lax.ppermute(value, axis, [(i, (i + step) % count) for i in range(count)])]
    convert_element_type x12 -> x0, local copies, waits for them, and re-layouts: 24.5 us -> none  [the longest x4 8.2 us: layer(): block[:, :ff_own].astype(F32)]
    dynamic_update_slice x12 -> x0, local copies, waits for them, and re-layouts: 11.2 us -> none  [the longest x4 4.43 us: layer(): lax.dynamic_update_slice_in_dim(grad_down_t, block[:, 2 * ff_own:].astype...]
    unnamed x301 -> x259, local copies, waits for them, and re-layouts: 54.9 us -> 49 us
  transfers between devices with their start and end apart: 112 -> 112, of which waited for: 47 -> 49; matrix products, arithmetic and copies ran while one was open for 41% -> 34% of each run, Pallas kernels for 0% -> 1%
where the time goes in v2:
time: 826 us; the launch traced here: 817 us
  waiting for transfers between devices  385 us (47%)
  matrix products  143 us (17%)
  local copies, waits for them, and re-layouts  98.6 us (12%)
  starting transfers between devices  93.8 us (11%)
  other arithmetic  87.7 us (11%)
    ppermute x112, waiting for transfers between devices, shift(): lax.ppermute(value, axis, [(i, (i + step) % count) for i in range(count)])  385 us
    ppermute x112, starting transfers between devices, shift(): lax.ppermute(value, axis, [(i, (i + step) % count) for i in range(count)])  93.8 us
    unnamed x259, local copies, waits for them, and re-layouts  49 us
    dot_general x15, matrix products, dot_t(): lax.dot_general(left, right, (((1,), (1,)), ((), ())), preferred_element_...  39.9 us
    dot_general x12, matrix products, tdot(): lax.dot_general(left, right, (((0,), (0,)), ((), ())), preferred_element_...  38.8 us
    convert_element_type x37, other arithmetic, add_rounded(): return (left.astype(F32) + right.astype(F32)).astype(left.dtype)  27.4 us
    concatenate x17, other arithmetic, gather_rows(): piece = jnp.concatenate(gather_ring(piece, axis), axis=0)  22.8 us
  transfers between devices with their start and end apart: 112, of which 49 were waited for; matrix products, arithmetic and copies ran while one was open for 34% of the time, Pallas kernels for 1%

profile of v2, /device:TPU:0, one launch (start us, length us, event | category | flops | bytes accessed | tf_op | source)
XLA Modules:
  0.0 816.6 jit_solution(5496331044495584277)
XLA Ops:
  8.6 8.0 collective-permute-done.2
  20.8 5.7 iota_compare_fusion
  29.4 17.0 %collective-permute-done.5 = bf16[64,3200]{1,0:T(8,128)(2,1)S(1)} collective-permute-done((bf16[64,3200]{1,0:T(8,128)(2,1)S(1)}, bf16[64,3200]{1,0:T(8,128)(2,1)S(1)}, u32[]{:S(2)}, u32[]{:S(2)}) %collective-permute-start.5) | collective-permute-done | bytes 409632 | tf_op jit(solution)/shard_map/ppermute | solution.py:81
  63.5 10.8 %collective-permute-done.8 = bf16[64,3200]{1,0:T(8,128)(2,1)S(1)} collective-permute-done((bf16[64,3200]{1,0:T(8,128)(2,1)S(1)}, bf16[64,3200]{1,0:T(8,128)(2,1)S(1)}, u32[]{:S(2)}, u32[]{:S(2)}) %collective-permute-start.8) | collective-permute-done | bytes 409632 | tf_op jit(solution)/shard_map/ppermute | solution.py:81
  90.1 11.5 %collective-permute-done.12 = bf16[64,3200]{1,0:T(8,128)(2,1)S(1)} collective-permute-done((bf16[64,3200]{1,0:T(8,128)(2,1)S(1)}, bf16[64,3200]{1,0:T(8,128)(2,1)S(1)}, u32[]{:S(2)}, u32[]{:S(2)}) %collective-permute-start.12) | collective-permute-done | bytes 409632 | tf_op jit(solution)/shard_map/ppermute | solution.py:81
  106.9 7.6 collective-permute-done.21
  134.7 4.6 multiply_convert_fusion.14
  217.5 5.3 collective-permute-done.68
  229.0 14.4 %collective-permute-done.41 = bf16[256,1536]{0,1:T(8,128)(2,1)S(1)} collective-permute-done((bf16[256,1536]{0,1:T(8,128)(2,1)}, bf16[256,1536]{0,1:T(8,128)(2,1)S(1)}, u32[]{:S(2)}, u32[]{:S(2)}) %collective-permute-start.41) | collective-permute-done | bytes 786464 | tf_op jit(solution)/shard_map/ppermute | solution.py:81
  245.9 14.3 %collective-permute-done.42 = bf16[256,1536]{0,1:T(8,128)(2,1)S(1)} collective-permute-done((bf16[256,1536]{0,1:T(8,128)(2,1)}, bf16[256,1536]{0,1:T(8,128)(2,1)S(1)}, u32[]{:S(2)}, u32[]{:S(2)}) %collective-permute-start.42) | collective-permute-done | bytes 786464 | tf_op jit(solution)/shard_map/ppermute | solution.py:81
  262.1 14.0 %collective-permute-done.43 = bf16[256,1536]{0,1:T(8,128)(2,1)S(1)} collective-permute-done((bf16[256,1536]{0,1:T(8,128)(2,1)}, bf16[256,1536]{0,1:T(8,128)(2,1)S(1)}, u32[]{:S(2)}, u32[]{:S(2)}) %collective-permute-start.43) | collective-permute-done | bytes 786464 | tf_op jit(solution)/shard_map/ppermute | solution.py:81
  277.1 13.8 %collective-permute-done.50 = bf16[128,2048]{1,0:T(8,128)(2,1)S(1)} collective-permute-done((bf16[128,2048]{1,0:T(8,128)(2,1)S(1)}, bf16[128,2048]{1,0:T(8,128)(2,1)S(1)}, u32[]{:S(2)}, u32[]{:S(2)}) %collective-permute-start.50) | collective-permute-done | bytes 524320 | tf_op jit(solution)/shard_map/ppermute | solution.py:81
  311.7 5.3 collective-permute-done.70
  321.9 6.3 collective-permute-done.60
  331.1 7.9 collective-permute-done.45
  397.1 9.6 %convolution_convert_fusion.12 = bf16[2048,512]{1,0:T(8,128)(2,1)} fusion(bf16[2048,2048]{1,0:T(8,128)(2,1)} %constant_dynamic-update-slice_fusion.28, bf16[2048,512]{0,1:T(8,128)(2,1)S(1)} %get-tuple-element.115), kind=kOutput, calls=%fused_computation.57 | convolution fusion | flops 4296015872 | bytes 12582912 | tf_op jit(solution)/shard_map/dot_general | solution.py:60
  407.9 9.5 %convolution_convert_fusion.11 = bf16[2048,512]{1,0:T(8,128)(2,1)} fusion(bf16[2048,2048]{1,0:T(8,128)(2,1)} %constant_dynamic-update-slice_fusion.28, bf16[2048,512]{0,1:T(8,128)(2,1)S(1)} %get-tuple-element.127), kind=kOutput, calls=%fused_computation.56 | convolution fusion | flops 4296015872 | bytes 12582912 | tf_op jit(solution)/shard_map/dot_general | solution.py:60
  417.4 5.6 collective-permute-done.49
  424.4 9.5 %convolution_convert_fusion.10 = bf16[2048,512]{1,0:T(8,128)(2,1)} fusion(bf16[2048,2048]{1,0:T(8,128)(2,1)} %constant_dynamic-update-slice_fusion.40, bf16[2048,512]{0,1:T(8,128)(2,1)S(1)} %get-tuple-element.159), kind=kOutput, calls=%fused_computation.55 | convolution fusion | flops 4296015872 | bytes 12582912 | tf_op jit(solution)/shard_map/dot_general | solution.py:60
  433.9 4.8 collective-permute-done.58
  440.1 6.8 convolution_convert_fusion
  446.9 6.7 collective-permute-done.67
  461.6 4.4 fusion.54
  468.0 5.1 fusion.5
  473.1 5.4 fusion.120
  478.6 5.8 fusion.14
  510.7 5.9 collective-permute-done.76
  532.3 7.2 collective-permute-done.106
  543.8 12.5 %collective-permute-done.108 = bf16[256,1536]{1,0:T(8,128)(2,1)} collective-permute-done((bf16[256,1536]{1,0:T(8,128)(2,1)}, bf16[256,1536]{1,0:T(8,128)(2,1)}, u32[]{:S(2)}, u32[]{:S(2)}) %collective-permute-start.108) | collective-permute-done | bytes 786464 | tf_op jit(solution)/shard_map/ppermute | solution.py:81
  562.3 9.6 %collective-permute-done.109 = bf16[256,1536]{1,0:T(8,128)(2,1)S(1)} collective-permute-done((bf16[256,1536]{1,0:T(8,128)(2,1)S(1)}, bf16[256,1536]{1,0:T(8,128)(2,1)S(1)}, u32[]{:S(2)}, u32[]{:S(2)}) %collective-permute-start.109) | collective-permute-done | bytes 786464 | tf_op jit(solution)/shard_map/ppermute | solution.py:81
  574.6 5.0 fusion.49
  586.7 17.1 %collective-permute-done.78 = bf16[128,3200]{1,0:T(8,128)(2,1)S(1)} collective-permute-done((bf16[128,3200]{1,0:T(8,128)(2,1)S(1)}, bf16[128,3200]{1,0:T(8,128)(2,1)S(1)}, u32[]{:S(2)}, u32[]{:S(2)}) %collective-permute-start.78) | collective-permute-done | bytes 819232 | tf_op jit(solution)/shard_map/ppermute | solution.py:81
  606.9 16.5 %collective-permute-done.94 = bf16[128,3200]{1,0:T(8,128)(2,1)S(1)} collective-permute-done((bf16[128,3200]{1,0:T(8,128)(2,1)S(1)}, bf16[128,3200]{1,0:T(8,128)(2,1)S(1)}, u32[]{:S(2)}, u32[]{:S(2)}) %collective-permute-start.94) | collective-permute-done | bytes 819232 | tf_op jit(solution)/shard_map/ppermute | solution.py:81
  624.2 10.3 %collective-permute-done.79 = bf16[64,3200]{1,0:T(8,128)(2,1)S(1)} collective-permute-done((bf16[64,3200]{1,0:T(8,128)(2,1)S(1)}, bf16[64,3200]{1,0:T(8,128)(2,1)S(1)}, u32[]{:S(2)}, u32[]{:S(2)}) %collective-permute-start.79) | collective-permute-done | bytes 409632 | tf_op jit(solution)/shard_map/ppermute | solution.py:81
  638.2 6.6 collective-permute-done.91
  645.0 5.6 collective-permute-done.88
  652.3 5.5 add_convert_fusion.1
  662.7 11.4 %collective-permute-done.92 = bf16[64,3200]{1,0:T(8,128)(2,1)} collective-permute-done((bf16[64,3200]{1,0:T(8,128)(2,1)}, bf16[64,3200]{1,0:T(8,128)(2,1)}, u32[]{:S(2)}, u32[]{:S(2)}) %collective-permute-start.92) | collective-permute-done | bytes 409632 | tf_op jit(solution)/shard_map/ppermute | solution.py:81
  678.4 11.2 %collective-permute-done.96 = bf16[64,3200]{1,0:T(8,128)(2,1)S(1)} collective-permute-done((bf16[64,3200]{1,0:T(8,128)(2,1)S(1)}, bf16[64,3200]{1,0:T(8,128)(2,1)S(1)}, u32[]{:S(2)}, u32[]{:S(2)}) %collective-permute-start.96) | collective-permute-done | bytes 409632 | tf_op jit(solution)/shard_map/ppermute | solution.py:81
  691.1 8.1 collective-permute-done.98
  700.1 8.2 collective-permute-done.100
  709.3 15.9 %collective-permute-done.80 = bf16[2,128,2048]{2,1,0:T(8,128)(2,1)S(1)} collective-permute-done((bf16[2,128,2048]{2,1,0:T(8,128)(2,1)S(1)}, bf16[2,128,2048]{2,1,0:T(8,128)(2,1)S(1)}, u32[]{:S(2)}, u32[]{:S(2)}) %collective-permute-start.80) | collective-permute-done | bytes 1048608 | tf_op jit(solution)/shard_map/ppermute | solution.py:81
  726.0 19.0 %collective-permute-done.81 = bf16[2,128,2048]{2,1,0:T(8,128)(2,1)S(1)} collective-permute-done((bf16[2,128,2048]{2,1,0:T(8,128)(2,1)S(1)}, bf16[2,128,2048]{2,1,0:T(8,128)(2,1)S(1)}, u32[]{:S(2)}, u32[]{:S(2)}) %collective-permute-start.81) | collective-permute-done | bytes 1048608 | tf_op jit(solution)/shard_map/ppermute | solution.py:81
  746.0 5.0 collective-permute-start.111
  764.0 18.4 %collective-permute-done.102 = bf16[64,2048]{1,0:T(8,128)(2,1)S(1)} collective-permute-done((bf16[64,2048]{1,0:T(8,128)(2,1)S(1)}, bf16[64,2048]{1,0:T(8,128)(2,1)S(1)}, u32[]{:S(2)}, u32[]{:S(2)}) %collective-permute-start.102) | collective-permute-done | bytes 262176 | tf_op jit(solution)/shard_map/ppermute | solution.py:81
  789.0 4.7 collective-permute-done.103
  794.9 8.8 %collective-permute-done.86 = bf16[128,2048]{1,0:T(8,128)(2,1)S(1)} collective-permute-done((bf16[128,2048]{1,0:T(8,128)(2,1)S(1)}, bf16[128,2048]{1,0:T(8,128)(2,1)S(1)}, u32[]{:S(2)}, u32[]{:S(2)}) %collective-permute-start.86) | collective-permute-done | bytes 524320 | tf_op jit(solution)/shard_map/ppermute | solution.py:81
  808.7 4.9 place_blocks.1
  (695 shorter events, 376.0 us)
Async XLA Ops:
  18.5 42.4 %collective-permute-start.3 = (bf16[128,3200]{1,0:T(8,128)(2,1)}, bf16[128,3200]{1,0:T(8,128)(2,1)}, u32[]{:S(2)}, u32[]{:S(2)}) collective-permute-start(bf16[128,3200]{1,0:T(8,128)(2,1)} %pad_maximum_fusion.22), channel_id=1, source_target_pairs={{0,2},{2,0},{1,3},{3,1},{4,6},{6,4},{5,7},{7,5},{8,10},{10,8},{9,1... | collective-permute-start | bytes 2457608 | tf_op jit(solution)/shard_map/ppermute | solution.py:81
  26.5 22.4 %collective-permute-start.1 = (bf16[64,3200]{1,0:T(8,128)(2,1)S(1)}, bf16[64,3200]{1,0:T(8,128)(2,1)S(1)}, u32[]{:S(2)}, u32[]{:S(2)}) collective-permute-start(bf16[64,3200]{1,0:T(8,128)(2,1)S(1)} %collective-permute-done), channel_id=1, source_target_pairs={{0,8},{8,16},{16,24},{24,0},{1,9},{9,17},{17,25},{25,1},{2,10},{10... | collective-permute-start | bytes 1228808 | tf_op jit(solution)/shard_map/ppermute | solution.py:81
  47.4 41.3 %collective-permute-start.6 = (bf16[128,3200]{1,0:T(8,128)(2,1)}, bf16[128,3200]{1,0:T(8,128)(2,1)}, u32[]{:S(2)}, u32[]{:S(2)}) collective-permute-start(bf16[128,3200]{1,0:T(8,128)(2,1)} %pad_maximum_fusion.23), channel_id=1, source_target_pairs={{0,4},{4,0},{1,5},{5,1},{2,6},{6,2},{3,7},{7,3},{8,12},{12,8},{9,1... | collective-permute-start | bytes 2457608 | tf_op jit(solution)/shard_map/ppermute | solution.py:81
  52.9 21.5 %collective-permute-start.8 = (bf16[64,3200]{1,0:T(8,128)(2,1)S(1)}, bf16[64,3200]{1,0:T(8,128)(2,1)S(1)}, u32[]{:S(2)}, u32[]{:S(2)}) collective-permute-start(bf16[64,3200]{1,0:T(8,128)(2,1)S(1)} %collective-permute-done.1), channel_id=1, source_target_pairs={{0,4},{4,0},{1,5},{5,1},{2,6},{6,2},{3,7},{7,3},{8,12},{12,8},{9,1... | collective-permute-start | bytes 1228808 | tf_op jit(solution)/shard_map/ppermute | solution.py:81
  60.9 26.2 %collective-permute-start.19 = (bf16[64,2048]{1,0:T(8,128)(2,1)S(1)}, bf16[64,2048]{1,0:T(8,128)(2,1)}, u32[]{:S(2)}, u32[]{:S(2)}) collective-permute-start(bf16[64,2048]{1,0:T(8,128)(2,1)S(1)} %copy-done.35), channel_id=1, source_target_pairs={{0,8},{8,16},{16,24},{24,0},{1,9},{9,17},{17,25},{25,1},{2,10},{10... | collective-permute-start | bytes 786440 | tf_op jit(solution)/shard_map/ppermute | solution.py:81
  63.5 59.0 %collective-permute-start.4 = (bf16[256,3200]{1,0:T(8,128)(2,1)}, bf16[256,3200]{1,0:T(8,128)(2,1)}, u32[]{:S(2)}, u32[]{:S(2)}) collective-permute-start(bf16[256,3200]{1,0:T(8,128)(2,1)} %pad_maximum_fusion.1), channel_id=1, source_target_pairs={{0,1},{1,0},{2,3},{3,2},{4,5},{5,4},{6,7},{7,6},{8,9},{9,8},{10,11... | collective-permute-start | bytes 4915208 | tf_op jit(solution)/shard_map/ppermute | solution.py:81
  75.4 40.0 %collective-permute-start.9 = (bf16[128,3200]{1,0:T(8,128)(2,1)}, bf16[128,3200]{1,0:T(8,128)(2,1)}, u32[]{:S(2)}, u32[]{:S(2)}) collective-permute-start(bf16[128,3200]{1,0:T(8,128)(2,1)} %pad_maximum_fusion.24), channel_id=1, source_target_pairs={{0,2},{2,0},{1,3},{3,1},{4,6},{6,4},{5,7},{7,5},{8,10},{10,8},{9,1... | collective-permute-start | bytes 2457608 | tf_op jit(solution)/shard_map/ppermute | solution.py:81
  90.0 36.4 %collective-permute-start.7 = (bf16[256,3200]{1,0:T(8,128)(2,1)S(1)}, bf16[256,3200]{1,0:T(8,128)(2,1)S(1)}, u32[]{:S(2)}, u32[]{:S(2)}) collective-permute-start(bf16[256,3200]{1,0:T(8,128)(2,1)S(1)} %pad_maximum_fusion.2), channel_id=1, source_target_pairs={{0,1},{1,0},{2,3},{3,2},{4,5},{5,4},{6,7},{7,6},{8,9},{9,8},{10,11... | collective-permute-start | bytes 4915208 | tf_op jit(solution)/shard_map/ppermute | solution.py:81
  114.4 76.7 %collective-permute-start.37 = (bf16[256,1536]{0,1:T(8,128)(2,1)}, bf16[256,1536]{0,1:T(8,128)(2,1)}, u32[]{:S(2)}, u32[]{:S(2)}) collective-permute-start(bf16[256,1536]{0,1:T(8,128)(2,1)} %pad_maximum_fusion.27), channel_id=1, source_target_pairs={{0,8},{8,16},{16,24},{24,0},{1,9},{9,17},{17,25},{25,1},{2,10},{10... | collective-permute-start | bytes 2359304 | tf_op jit(solution)/shard_map/ppermute | solution.py:81
  115.4 76.3 %collective-permute-start.38 = (bf16[256,1536]{0,1:T(8,128)(2,1)}, bf16[256,1536]{0,1:T(8,128)(2,1)}, u32[]{:S(2)}, u32[]{:S(2)}) collective-permute-start(bf16[256,1536]{0,1:T(8,128)(2,1)} %pad_maximum_fusion.28), channel_id=1, source_target_pairs={{0,16},{8,24},{16,0},{24,8},{1,17},{9,25},{17,1},{25,9},{2,18},{10... | collective-permute-start | bytes 2359304 | tf_op jit(solution)/shard_map/ppermute | solution.py:81
  119.9 73.7 %collective-permute-start.39 = (bf16[256,1536]{0,1:T(8,128)(2,1)}, bf16[256,1536]{0,1:T(8,128)(2,1)}, u32[]{:S(2)}, u32[]{:S(2)}) collective-permute-start(bf16[256,1536]{0,1:T(8,128)(2,1)} %pad_maximum_fusion.29), channel_id=1, source_target_pairs={{0,24},{8,0},{16,8},{24,16},{1,25},{9,1},{17,9},{25,17},{2,26},{10... | collective-permute-start | bytes 2359304 | tf_op jit(solution)/shard_map/ppermute | solution.py:81
  149.6 24.3 %collective-permute-start.28 = (bf16[64,2048]{1,0:T(8,128)(2,1)}, bf16[64,2048]{1,0:T(8,128)(2,1)S(1)}, u32[]{:S(2)}, u32[]{:S(2)}) collective-permute-start(bf16[64,2048]{1,0:T(8,128)(2,1)} %collective-permute-done.20), channel_id=1, source_target_pairs={{0,4},{4,0},{1,5},{5,1},{2,6},{6,2},{3,7},{7,3},{8,12},{12,8},{9,1... | collective-permute-start | bytes 786440 | tf_op jit(solution)/shard_map/ppermute | solution.py:81
  193.7 32.5 %collective-permute-start.40 = (bf16[256,1536]{0,1:T(8,128)(2,1)S(1)}, bf16[256,1536]{0,1:T(8,128)(2,1)S(1)}, u32[]{:S(2)}, u32[]{:S(2)}) collective-permute-start(bf16[256,1536]{0,1:T(8,128)(2,1)S(1)} %copy-done.26), channel_id=1, source_target_pairs={{0,4},{4,0},{1,5},{5,1},{2,6},{6,2},{3,7},{7,3},{8,12},{12,8},{9,1... | collective-permute-start | bytes 2359304 | tf_op jit(solution)/shard_map/ppermute | solution.py:81
  206.5 39.4 %collective-permute-start.34 = (bf16[128,2048]{1,0:T(8,128)(2,1)S(1)}, bf16[128,2048]{1,0:T(8,128)(2,1)S(1)}, u32[]{:S(2)}, u32[]{:S(2)}) collective-permute-start(bf16[128,2048]{1,0:T(8,128)(2,1)S(1)} %bitcast.210), channel_id=1, source_target_pairs={{0,8},{8,16},{16,24},{24,0},{1,9},{9,17},{17,25},{25,1},{2,10},{10... | collective-permute-start | bytes 1572872 | tf_op jit(solution)/shard_map/ppermute | solution.py:81
  209.3 67.1 %collective-permute-start.33 = (bf16[256,2048]{1,0:T(8,128)(2,1)S(1)}, bf16[256,2048]{1,0:T(8,128)(2,1)S(1)}, u32[]{:S(2)}, u32[]{:S(2)}) collective-permute-start(bf16[256,2048]{1,0:T(8,128)(2,1)S(1)} %pad_maximum_fusion.12), channel_id=1, source_target_pairs={{0,1},{1,0},{2,3},{3,2},{4,5},{5,4},{6,7},{7,6},{8,9},{9,8},{10,11... | collective-permute-start | bytes 3145736 | tf_op jit(solution)/shard_map/ppermute | solution.py:81
  212.4 78.6 %collective-permute-start.30 = (bf16[256,2048]{1,0:T(8,128)(2,1)S(1)}, bf16[256,2048]{1,0:T(8,128)(2,1)S(1)}, u32[]{:S(2)}, u32[]{:S(2)}) collective-permute-start(bf16[256,2048]{1,0:T(8,128)(2,1)S(1)} %pad_maximum_fusion.11), channel_id=1, source_target_pairs={{0,1},{1,0},{2,3},{3,2},{4,5},{5,4},{6,7},{7,6},{8,9},{9,8},{10,11... | collective-permute-start | bytes 3145736 | tf_op jit(solution)/shard_map/ppermute | solution.py:81
  226.1 34.1 %collective-permute-start.42 = (bf16[256,1536]{0,1:T(8,128)(2,1)}, bf16[256,1536]{0,1:T(8,128)(2,1)S(1)}, u32[]{:S(2)}, u32[]{:S(2)}) collective-permute-start(bf16[256,1536]{0,1:T(8,128)(2,1)} %collective-permute-done.38), channel_id=1, source_target_pairs={{0,4},{4,0},{1,5},{5,1},{2,6},{6,2},{3,7},{7,3},{8,12},{12,8},{9,1... | collective-permute-start | bytes 2359304 | tf_op jit(solution)/shard_map/ppermute | solution.py:81
  243.4 32.8 %collective-permute-start.43 = (bf16[256,1536]{0,1:T(8,128)(2,1)}, bf16[256,1536]{0,1:T(8,128)(2,1)S(1)}, u32[]{:S(2)}, u32[]{:S(2)}) collective-permute-start(bf16[256,1536]{0,1:T(8,128)(2,1)} %collective-permute-done.39), channel_id=1, source_target_pairs={{0,4},{4,0},{1,5},{5,1},{2,6},{6,2},{3,7},{7,3},{8,12},{12,8},{9,1... | collective-permute-start | bytes 2359304 | tf_op jit(solution)/shard_map/ppermute | solution.py:81
  245.9 45.7 %collective-permute-start.27 = (bf16[256,2048]{1,0:T(8,128)(2,1)S(1)}, bf16[256,2048]{1,0:T(8,128)(2,1)S(1)}, u32[]{:S(2)}, u32[]{:S(2)}) collective-permute-start(bf16[256,2048]{1,0:T(8,128)(2,1)S(1)} %pad_maximum_fusion.10), channel_id=1, source_target_pairs={{0,1},{1,0},{2,3},{3,2},{4,5},{5,4},{6,7},{7,6},{8,9},{9,8},{10,11... | collective-permute-start | bytes 3145736 | tf_op jit(solution)/shard_map/ppermute | solution.py:81
  276.4 29.4 %collective-permute-start.69 = (bf16[256,2048]{1,0:T(8,128)(2,1)S(1)}, bf16[256,2048]{1,0:T(8,128)(2,1)S(1)}, u32[]{:S(2)}, u32[]{:S(2)}) collective-permute-start(bf16[256,2048]{1,0:T(8,128)(2,1)S(1)} %pad_maximum_fusion.19), channel_id=1, source_target_pairs={{0,1},{1,0},{2,3},{3,2},{4,5},{5,4},{6,7},{7,6},{8,9},{9,8},{10,11... | collective-permute-start | bytes 3145736 | tf_op jit(solution)/shard_map/ppermute | solution.py:81
  290.9 37.4 %collective-permute-start.36 = (bf16[256,2048]{1,0:T(8,128)(2,1)S(1)}, bf16[256,2048]{1,0:T(8,128)(2,1)S(1)}, u32[]{:S(2)}, u32[]{:S(2)}) collective-permute-start(bf16[256,2048]{1,0:T(8,128)(2,1)S(1)} %pad_maximum_fusion.13), channel_id=1, source_target_pairs={{0,1},{1,0},{2,3},{3,2},{4,5},{5,4},{6,7},{7,6},{8,9},{9,8},{10,11... | collective-permute-start | bytes 3145736 | tf_op jit(solution)/shard_map/ppermute | solution.py:81
  305.8 37.7 %collective-permute-start.52 = (bf16[256,2048]{1,0:T(8,128)(2,1)S(1)}, bf16[256,2048]{1,0:T(8,128)(2,1)S(1)}, u32[]{:S(2)}, u32[]{:S(2)}) collective-permute-start(bf16[256,2048]{1,0:T(8,128)(2,1)S(1)} %pad_maximum_fusion.15), channel_id=1, source_target_pairs={{0,1},{1,0},{2,3},{3,2},{4,5},{5,4},{6,7},{7,6},{8,9},{9,8},{10,11... | collective-permute-start | bytes 3145736 | tf_op jit(solution)/shard_map/ppermute | solution.py:81
  307.5 20.7 %collective-permute-start.60 = (bf16[128,2048]{1,0:T(8,128)(2,1)S(1)}, bf16[128,2048]{1,0:T(8,128)(2,1)S(1)}, u32[]{:S(2)}, u32[]{:S(2)}) collective-permute-start(bf16[128,2048]{1,0:T(8,128)(2,1)S(1)} %collective-permute-done.59), channel_id=1, source_target_pairs={{0,2},{2,0},{1,3},{3,1},{4,6},{6,4},{5,7},{7,5},{8,10},{10,8},{9,1... | collective-permute-start | bytes 1572872 | tf_op jit(solution)/shard_map/ppermute | solution.py:81
  317.1 29.4 %collective-permute-start.71 = (bf16[256,2048]{1,0:T(8,128)(2,1)S(1)}, bf16[256,2048]{1,0:T(8,128)(2,1)S(1)}, u32[]{:S(2)}, u32[]{:S(2)}) collective-permute-start(bf16[256,2048]{1,0:T(8,128)(2,1)S(1)} %pad_maximum_fusion.20), channel_id=1, source_target_pairs={{0,1},{1,0},{2,3},{3,2},{4,5},{5,4},{6,7},{7,6},{8,9},{9,8},{10,11... | collective-permute-start | bytes 3145736 | tf_op jit(solution)/shard_map/ppermute | solution.py:81
  328.3 32.5 %collective-permute-start.61 = (bf16[256,2048]{1,0:T(8,128)(2,1)S(1)}, bf16[256,2048]{1,0:T(8,128)(2,1)S(1)}, u32[]{:S(2)}, u32[]{:S(2)}) collective-permute-start(bf16[256,2048]{1,0:T(8,128)(2,1)S(1)} %pad_maximum_fusion.17), channel_id=1, source_target_pairs={{0,1},{1,0},{2,3},{3,2},{4,5},{5,4},{6,7},{7,6},{8,9},{9,8},{10,11... | collective-permute-start | bytes 3145736 | tf_op jit(solution)/shard_map/ppermute | solution.py:81
  339.1 22.8 %collective-permute-start.46 = (bf16[256,2048]{1,0:T(8,128)(2,1)S(1)}, bf16[256,2048]{1,0:T(8,128)(2,1)S(1)}, u32[]{:S(2)}, u32[]{:S(2)}) collective-permute-start(bf16[256,2048]{1,0:T(8,128)(2,1)S(1)} %pad_maximum_fusion.14), channel_id=1, source_target_pairs={{0,1},{1,0},{2,3},{3,2},{4,5},{5,4},{6,7},{7,6},{8,9},{9,8},{10,11... | collective-permute-start | bytes 3145736 | tf_op jit(solution)/shard_map/ppermute | solution.py:81
  354.9 21.1 %collective-permute-start.72 = (bf16[256,2048]{1,0:T(8,128)(2,1)}, bf16[256,2048]{1,0:T(8,128)(2,1)S(1)}, u32[]{:S(2)}, u32[]{:S(2)}) collective-permute-start(bf16[256,2048]{1,0:T(8,128)(2,1)} %slice.605), channel_id=1, source_target_pairs={{0,1},{1,0},{2,3},{3,2},{4,5},{5,4},{6,7},{7,6},{8,9},{9,8},{10,11... | collective-permute-start | bytes 3145736 | tf_op jit(solution)/shard_map/ppermute | solution.py:81
  376.5 70.4 %collective-permute-start.73 = (bf16[128,2048]{1,0:T(8,128)(2,1)S(1)}, bf16[128,2048]{1,0:T(8,128)(2,1)S(1)}, u32[]{:S(2)}, u32[]{:S(2)}) collective-permute-start(bf16[128,2048]{1,0:T(8,128)(2,1)S(1)} %slice.607), channel_id=1, source_target_pairs={{0,2},{2,0},{1,3},{3,1},{4,6},{6,4},{5,7},{7,5},{8,10},{10,8},{9,1... | collective-permute-start | bytes 1572872 | tf_op jit(solution)/shard_map/ppermute | solution.py:81
  383.7 23.2 %collective-permute-start.56 = (bf16[256,2048]{1,0:T(8,128)(2,1)S(1)}, bf16[256,2048]{1,0:T(8,128)(2,1)S(1)}, u32[]{:S(2)}, u32[]{:S(2)}) collective-permute-start(bf16[256,2048]{1,0:T(8,128)(2,1)S(1)} %slice.593), channel_id=1, source_target_pairs={{0,1},{1,0},{2,3},{3,2},{4,5},{5,4},{6,7},{7,6},{8,9},{9,8},{10,11... | collective-permute-start | bytes 3145736 | tf_op jit(solution)/shard_map/ppermute | solution.py:81
  395.7 27.6 %collective-permute-start.65 = (bf16[256,2048]{1,0:T(8,128)(2,1)S(1)}, bf16[256,2048]{1,0:T(8,128)(2,1)S(1)}, u32[]{:S(2)}, u32[]{:S(2)}) collective-permute-start(bf16[256,2048]{1,0:T(8,128)(2,1)S(1)} %slice.599), channel_id=1, source_target_pairs={{0,1},{1,0},{2,3},{3,2},{4,5},{5,4},{6,7},{7,6},{8,9},{9,8},{10,11... | collective-permute-start | bytes 3145736 | tf_op jit(solution)/shard_map/ppermute | solution.py:81
  492.5 159.5 %collective-permute-start.74 = (bf16[4,256,2048]{2,1,0:T(8,128)(2,1)}, bf16[4,256,2048]{2,1,0:T(8,128)(2,1)}, u32[]{:S(2)}, u32[]{:S(2)}) collective-permute-start(bf16[4,256,2048]{2,1,0:T(8,128)(2,1)} %slice.609), channel_id=1, source_target_pairs={{0,1},{1,0},{2,3},{3,2},{4,5},{5,4},{6,7},{7,6},{8,9},{9,8},{10,11... | collective-permute-start | bytes 12582920 | tf_op jit(solution)/shard_map/ppermute | solution.py:81
  496.3 161.6 %collective-permute-start.97 = (bf16[4,256,2048]{2,1,0:T(8,128)(2,1)}, bf16[4,256,2048]{2,1,0:T(8,128)(2,1)}, u32[]{:S(2)}, u32[]{:S(2)}) collective-permute-start(bf16[4,256,2048]{2,1,0:T(8,128)(2,1)} %slice.655), channel_id=1, source_target_pairs={{0,1},{1,0},{2,3},{3,2},{4,5},{5,4},{6,7},{7,6},{8,9},{9,8},{10,11... | collective-permute-start | bytes 12582920 | tf_op jit(solution)/shard_map/ppermute | solution.py:81
  501.9 257.4 %collective-permute-start.105 = (bf16[256,1536]{1,0:T(8,128)(2,1)}, bf16[256,1536]{1,0:T(8,128)(2,1)}, u32[]{:S(2)}, u32[]{:S(2)}) collective-permute-start(bf16[256,1536]{1,0:T(8,128)(2,1)} %pad_maximum_fusion.31), channel_id=1, source_target_pairs={{0,4},{4,0},{1,5},{5,1},{2,6},{6,2},{3,7},{7,3},{8,12},{12,8},{9,1... | collective-permute-start | bytes 2359304 | tf_op jit(solution)/shard_map/ppermute | solution.py:81
  504.7 34.8 %collective-permute-start.106 = (bf16[256,1536]{1,0:T(8,128)(2,1)}, bf16[256,1536]{1,0:T(8,128)(2,1)}, u32[]{:S(2)}, u32[]{:S(2)}) collective-permute-start(bf16[256,1536]{1,0:T(8,128)(2,1)} %pad_maximum_fusion.32), channel_id=1, source_target_pairs={{0,4},{4,0},{1,5},{5,1},{2,6},{6,2},{3,7},{7,3},{8,12},{12,8},{9,1... | collective-permute-start | bytes 2359304 | tf_op jit(solution)/shard_map/ppermute | solution.py:81
  516.6 39.7 %collective-permute-start.108 = (bf16[256,1536]{1,0:T(8,128)(2,1)}, bf16[256,1536]{1,0:T(8,128)(2,1)}, u32[]{:S(2)}, u32[]{:S(2)}) collective-permute-start(bf16[256,1536]{1,0:T(8,128)(2,1)} %pad_maximum_fusion.33), channel_id=1, source_target_pairs={{0,4},{4,0},{1,5},{5,1},{2,6},{6,2},{3,7},{7,3},{8,12},{12,8},{9,1... | collective-permute-start | bytes 2359304 | tf_op jit(solution)/shard_map/ppermute | solution.py:81
  539.5 32.4 %collective-permute-start.109 = (bf16[256,1536]{1,0:T(8,128)(2,1)S(1)}, bf16[256,1536]{1,0:T(8,128)(2,1)S(1)}, u32[]{:S(2)}, u32[]{:S(2)}) collective-permute-start(bf16[256,1536]{1,0:T(8,128)(2,1)S(1)} %copy-done.66), channel_id=1, source_target_pairs={{0,4},{4,0},{1,5},{5,1},{2,6},{6,2},{3,7},{7,3},{8,12},{12,8},{9,1... | collective-permute-start | bytes 2359304 | tf_op jit(solution)/shard_map/ppermute | solution.py:81
  556.3 23.3 %collective-permute-start.77 = (bf16[256,3200]{1,0:T(8,128)(2,1)S(1)}, bf16[256,3200]{1,0:T(8,128)(2,1)S(1)}, u32[]{:S(2)}, u32[]{:S(2)}) collective-permute-start(bf16[256,3200]{1,0:T(8,128)(2,1)S(1)} %slice.618), channel_id=1, source_target_pairs={{0,1},{1,0},{2,3},{3,2},{4,5},{5,4},{6,7},{7,6},{8,9},{9,8},{10,11... | collective-permute-start | bytes 4915208 | tf_op jit(solution)/shard_map/ppermute | solution.py:81
  606.1 30.3 %collective-permute-start.83 = (bf16[128,3200]{1,0:T(8,128)(2,1)S(1)}, bf16[128,3200]{1,0:T(8,128)(2,1)S(1)}, u32[]{:S(2)}, u32[]{:S(2)}) collective-permute-start(bf16[128,3200]{1,0:T(8,128)(2,1)S(1)} %slice.633), channel_id=1, source_target_pairs={{0,2},{2,0},{1,3},{3,1},{4,6},{6,4},{5,7},{7,5},{8,10},{10,8},{9,1... | collective-permute-start | bytes 2457608 | tf_op jit(solution)/shard_map/ppermute | solution.py:81
  644.8 162.1 %collective-permute-start.107 = (bf16[256,1536]{1,0:T(8,128)(2,1)}, bf16[256,1536]{1,0:T(8,128)(2,1)}, u32[]{:S(2)}, u32[]{:S(2)}) collective-permute-start(bf16[256,1536]{1,0:T(8,128)(2,1)} %add_convert_fusion.20), channel_id=1, source_target_pairs={{0,24},{8,0},{16,8},{24,16},{1,25},{9,1},{17,9},{25,17},{2,26},{10... | collective-permute-start | bytes 2359304 | tf_op jit(solution)/shard_map/ppermute | solution.py:81
  652.1 24.6 %collective-permute-start.84 = (bf16[64,3200]{1,0:T(8,128)(2,1)}, bf16[64,3200]{1,0:T(8,128)(2,1)}, u32[]{:S(2)}, u32[]{:S(2)}) collective-permute-start(bf16[64,3200]{1,0:T(8,128)(2,1)} %slice.635), channel_id=1, source_target_pairs={{0,4},{4,0},{1,5},{5,1},{2,6},{6,2},{3,7},{7,3},{8,12},{12,8},{9,1... | collective-permute-start | bytes 1228808 | tf_op jit(solution)/shard_map/ppermute | solution.py:81
  675.8 23.4 %collective-permute-start.98 = (bf16[2,128,2048]{2,1,0:T(8,128)(2,1)S(1)}, bf16[2,128,2048]{2,1,0:T(8,128)(2,1)S(1)}, u32[]{:S(2)}, u32[]{:S(2)}) collective-permute-start(bf16[2,128,2048]{2,1,0:T(8,128)(2,1)S(1)} %slice.657), channel_id=1, source_target_pairs={{0,2},{2,0},{1,3},{3,1},{4,6},{6,4},{5,7},{7,5},{8,10},{10,8},{9,1... | collective-permute-start | bytes 3145736 | tf_op jit(solution)/shard_map/ppermute | solution.py:81
  677.6 129.3 %collective-permute-start.110 = (bf16[256,1536]{1,0:T(8,128)(2,1)S(1)}, bf16[256,1536]{1,0:T(8,128)(2,1)S(1)}, u32[]{:S(2)}, u32[]{:S(2)}) collective-permute-start(bf16[256,1536]{1,0:T(8,128)(2,1)S(1)} %copy-done.67), channel_id=1, source_target_pairs={{0,16},{8,24},{16,0},{24,8},{1,17},{9,25},{17,1},{25,9},{2,18},{10... | collective-permute-start | bytes 2359304 | tf_op jit(solution)/shard_map/ppermute | solution.py:81
  699.2 26.0 %collective-permute-start.80 = (bf16[2,128,2048]{2,1,0:T(8,128)(2,1)S(1)}, bf16[2,128,2048]{2,1,0:T(8,128)(2,1)S(1)}, u32[]{:S(2)}, u32[]{:S(2)}) collective-permute-start(bf16[2,128,2048]{2,1,0:T(8,128)(2,1)S(1)} %fusion.135), channel_id=1, source_target_pairs={{0,2},{2,0},{1,3},{3,1},{4,6},{6,4},{5,7},{7,5},{8,10},{10,8},{9,1... | collective-permute-start | bytes 3145736 | tf_op jit(solution)/shard_map/ppermute | solution.py:81
  708.3 36.7 %collective-permute-start.81 = (bf16[2,128,2048]{2,1,0:T(8,128)(2,1)S(1)}, bf16[2,128,2048]{2,1,0:T(8,128)(2,1)S(1)}, u32[]{:S(2)}, u32[]{:S(2)}) collective-permute-start(bf16[2,128,2048]{2,1,0:T(8,128)(2,1)S(1)} %slice.479), channel_id=1, source_target_pairs={{0,2},{2,0},{1,3},{3,1},{4,6},{6,4},{5,7},{7,5},{8,10},{10,8},{9,1... | collective-permute-start | bytes 3145736 | tf_op jit(solution)/shard_map/ppermute | solution.py:81
  725.2 20.8 %collective-permute-start.99 = (bf16[2,64,2048]{2,1,0:T(8,128)(2,1)S(1)}, bf16[2,64,2048]{2,1,0:T(8,128)(2,1)S(1)}, u32[]{:S(2)}, u32[]{:S(2)}) collective-permute-start(bf16[2,64,2048]{2,1,0:T(8,128)(2,1)S(1)} %slice.659), channel_id=1, source_target_pairs={{0,4},{4,0},{1,5},{5,1},{2,6},{6,2},{3,7},{7,3},{8,12},{12,8},{9,1... | collective-permute-start | bytes 1572872 | tf_op jit(solution)/shard_map/ppermute | solution.py:81
  746.0 60.9 %collective-permute-start.111 = (bf16[256,1536]{1,0:T(8,128)(2,1)S(1)}, bf16[256,1536]{1,0:T(8,128)(2,1)S(1)}, u32[]{:S(2)}, u32[]{:S(2)}) collective-permute-start(bf16[256,1536]{1,0:T(8,128)(2,1)S(1)} %copy-done.68), channel_id=1, source_target_pairs={{0,8},{8,16},{16,24},{24,0},{1,9},{9,17},{17,25},{25,1},{2,10},{10... | collective-permute-start | bytes 2359304 | tf_op jit(solution)/shard_map/ppermute | solution.py:81
  754.8 30.8 %collective-permute-start.85 = (bf16[128,2048]{1,0:T(8,128)(2,1)S(1)}, bf16[128,2048]{1,0:T(8,128)(2,1)S(1)}, u32[]{:S(2)}, u32[]{:S(2)}) collective-permute-start(bf16[128,2048]{1,0:T(8,128)(2,1)S(1)} %get-tuple-element.80), channel_id=1, source_target_pairs={{0,8},{8,16},{16,24},{24,0},{1,9},{9,17},{17,25},{25,1},{2,10},{10... | collective-permute-start | bytes 1572872 | tf_op jit(solution)/shard_map/ppermute | solution.py:81
  759.3 23.1 %collective-permute-start.102 = (bf16[64,2048]{1,0:T(8,128)(2,1)S(1)}, bf16[64,2048]{1,0:T(8,128)(2,1)S(1)}, u32[]{:S(2)}, u32[]{:S(2)}) collective-permute-start(bf16[64,2048]{1,0:T(8,128)(2,1)S(1)} %slice_bitcast_fusion.4), channel_id=1, source_target_pairs={{0,8},{8,16},{16,24},{24,0},{1,9},{9,17},{17,25},{25,1},{2,10},{10... | collective-permute-start | bytes 786440 | tf_op jit(solution)/shard_map/ppermute | solution.py:81
  (173 other events, 1882.1 us)
